TPU v7x, 32 devices: a whole 2x2x4 slice. The times are simulated.
32 devices in a mesh: atoms: 8 (over z, y), chan: 4 (over x, core).
Axes of the slice: x: 2, y: 2, z: 4, core: 2. Of those that a mesh axis runs over, the one named last changes fastest.
Arguments:
- node_x: bfloat16 [49, 128, 512], P(None, 'chan', 'atoms'), may hold values from -6 to 6
- cotangent: bfloat16 [49, 128, 512], P(None, 'chan', 'atoms'), may hold values from -6 to 6
- rotation: bfloat16 [235, 4096], P(None, 'atoms'), may hold values from -2.5 to 2.5
- envelope: float32 [4096], P('atoms'), may hold values from 0.2 to 1
- source: int32 [4096], P('atoms'), may hold values from 0 to 127, as said below
- target: int32 [4096], P('atoms'), may hold values from 0 to 63
- edge_count: int32 [8], P('atoms'), may hold values from 128 to 512, as said below
- send_index: int32 [8, 8, 8], P('atoms'), may hold values from 0 to 63
- halo_count: int32 [8, 8], P(None, 'atoms'), may hold values from 0 to 8, as said below
- weight_zero: bfloat16 [7, 128, 7, 128], P(None, 'chan'), may hold values from -0.1875 to 0.1875
- weight_one: bfloat16 [2, 6, 128, 6, 128], P(None, None, 'chan'), may hold values from -0.15625 to 0.15625
- weight_two: bfloat16 [2, 5, 128, 5, 128], P(None, None, 'chan'), may hold values from -0.15625 to 0.15625
Outputs:
- grad_x: float32 [49, 128, 512], P(None, 'chan', 'atoms')
- grad_weight_zero: float32 [7, 128, 7, 128], P(None, 'chan', None, 'atoms')
- grad_weight_one: float32 [2, 6, 128, 6, 128], P(None, None, 'chan', None, 'atoms')
- grad_weight_two: float32 [2, 5, 128, 5, 128], P(None, None, 'chan', None, 'atoms')
Inputs may be any that keep to these rules, and one draw needn't show every extreme that they name: `edge_count`: at least 128 slots of each partition are live, and some partition has all 512 slots live in every draw; live slots come first. `halo_count`: A partition sends nothing to itself and between 4 and 8 atoms to every other partition; partitions whose indices differ by one, cyclically, exchange exactly 8. `source`: A value of 64 or more names slot j of sender p with p other than the edge's own partition and j below halo_count[p, own partition].
All inputs are finite; a program needn't handle non-finite values.
Results may differ from a plain program's by a relative error of at most 0.005.
Values may be sent and summed in bfloat16 or wider, within the bound.
A program may use at most 128 MiB of HBM per device.

v0:
```python
import math

import jax
import jax.numpy as jnp
from jax import lax
from jax.sharding import PartitionSpec as P

BLOCK = 512


def frame_pairs():
    listing = [(degree, 0) for degree in range(7)]
    for order in (1, 2):
        listing = listing + [(degree, order) for degree in range(order, 7)]
        listing = listing + [(degree, -order) for degree in range(order, 7)]
    return listing


def rotate_in(packed, feature):
    pieces = []
    offset = 0
    for degree in range(7):
        reach = min(degree, 2)
        height = 2 * reach + 1
        breadth = 2 * degree + 1
        matrix = packed[offset : offset + height * breadth].reshape(
            height, breadth, packed.shape[1]
        )
        offset = offset + height * breadth
        part_in = feature[degree * degree : degree * degree + breadth]
        pieces.append(jnp.einsum("rke,kce->rce", matrix, part_in))
    return jnp.stack([pieces[degree][min(degree, 2) + order] for degree, order in frame_pairs()])


def rotate_out(packed, framed):
    places = {pair: index for index, pair in enumerate(frame_pairs())}
    pieces = []
    offset = 0
    for degree in range(7):
        reach = min(degree, 2)
        height = 2 * reach + 1
        breadth = 2 * degree + 1
        matrix = packed[offset : offset + height * breadth].reshape(
            height, breadth, packed.shape[1]
        )
        offset = offset + height * breadth
        stacked = jnp.stack([framed[places[degree, order]] for order in range(-reach, reach + 1)])
        pieces.append(jnp.einsum("rke,rce->kce", matrix, stacked))
    return jnp.concatenate(pieces, axis=0)


def contract(weight, grads):
    first, inner, second, other = weight.shape
    count = grads.shape[2]
    product = jnp.dot(
        weight.reshape(first * inner, second * other),
        grads.reshape(second * other, count),
        preferred_element_type=jnp.float32,
    )
    return product.reshape(first, inner, count)


def outer_sum(rotated, grads):
    first, inner, count = rotated.shape
    second, other = (grads.shape[0], grads.shape[1])
    product = lax.dot_general(
        rotated.reshape(first * inner, count),
        grads.reshape(second * other, count),
        (((1,), (1,)), ((), ())),
        preferred_element_type=jnp.float32,
    )
    return product.reshape(first, inner, second, other)


def frame_backward(rotated, edge_grad, weight_zero, weight_one, weight_two):
    spans = ((0, 7), (7, 13), (13, 19), (19, 24), (24, 29))
    hpart = [rotated[start:stop] for start, stop in spans]
    gpart = [edge_grad[start:stop] for start, stop in spans]
    backs = [contract(weight_zero, gpart[0])]
    grad_zero = outer_sum(hpart[0], gpart[0])
    grads = []
    for weight, plus, minus in ((weight_one, 1, 2), (weight_two, 3, 4)):
        real_part = weight[0]
        imag_part = weight[1]
        backs.append(contract(real_part, gpart[plus]) + contract(imag_part, gpart[minus]))
        backs.append(contract(real_part, gpart[minus]) - contract(imag_part, gpart[plus]))
        grad_real = outer_sum(hpart[plus], gpart[plus]) + outer_sum(hpart[minus], gpart[minus])
        grad_imag = outer_sum(hpart[plus], gpart[minus]) - outer_sum(hpart[minus], gpart[plus])
        grads.append(jnp.stack([grad_real, grad_imag]))
    return (jnp.concatenate(backs, axis=0), grad_zero, grads[0], grads[1])


def on_device(
    node_x,
    cotangent,
    rotation,
    envelope,
    source,
    target,
    edge_count,
    send_index,
    halo_count,
    weight_zero,
    weight_one,
    weight_two,
):
    parts = lax.axis_size("atoms")
    channels = node_x.shape[1]
    atom_dev = node_x.shape[2]
    halo = send_index.shape[2]
    edge_dev = source.shape[0]
    sends = send_index[0].reshape(parts * halo)
    outgoing = (
        node_x[:, :, sends]
        .reshape(49, channels, parts, halo)
        .transpose(2, 0, 1, 3)
        .reshape(parts, 49, channels * halo)
    )
    incoming = lax.all_to_all(outgoing, "atoms", split_axis=0, concat_axis=0, tiled=True)
    received = (
        incoming.reshape(parts, 49, channels, halo)
        .transpose(1, 2, 0, 3)
        .reshape(49, channels, parts * halo)
    )
    table = jnp.concatenate([node_x, received], axis=2)
    live_count = edge_count[0]
    counts_in = halo_count[:, 0]
    halo_slot = jnp.maximum(source - atom_dev, 0)
    sender = halo_slot // halo
    within = halo_slot % halo
    allowed = jnp.sum(
        jnp.where(
            sender[:, None] == jnp.arange(parts, dtype=jnp.int32)[None, :], counts_in[None, :], 0
        ),
        axis=1,
    )
    usable = (source < atom_dev) | (within < allowed)
    alive = (jnp.arange(edge_dev, dtype=jnp.int32) < live_count) & usable
    radial = envelope * alive.astype(jnp.float32)
    whole_packed = rotation.astype(jnp.float32)
    local_grad = (
        rotate_in(whole_packed, cotangent[:, :, target].astype(jnp.float32)) * radial
    ).astype(jnp.bfloat16)
    gathered_grad = lax.all_gather(local_grad, "chan", axis=1, tiled=True)

    def one_block(turn, carry):
        grad_table, grad_zero, grad_one, grad_two = carry
        packed = rotation.astype(jnp.float32)
        rotated = rotate_in(packed, table[:, :, source].astype(jnp.float32)).astype(jnp.bfloat16)
        frame_back, add_zero, add_one, add_two = frame_backward(
            rotated, gathered_grad, weight_zero, weight_one, weight_two
        )
        grad_table = grad_table.at[:, :, source].add(rotate_out(packed, frame_back))
        return (grad_table, grad_zero + add_zero, grad_one + add_one, grad_two + add_two)

    start_carry = (
        jnp.zeros((49, channels, atom_dev + parts * halo), jnp.float32),
        jnp.zeros((7, channels, 7, weight_zero.shape[3]), jnp.float32),
        jnp.zeros((2, 6, channels, 6, weight_one.shape[4]), jnp.float32),
        jnp.zeros((2, 5, channels, 5, weight_two.shape[4]), jnp.float32),
    )
    turns = edge_dev // BLOCK
    grad_table, grad_zero, grad_one, grad_two = lax.fori_loop(0, turns, one_block, start_carry)
    own_grad = grad_table[:, :, :atom_dev]
    halo_grad = (
        grad_table[:, :, atom_dev:]
        .reshape(49, channels, parts, halo)
        .transpose(2, 0, 1, 3)
        .reshape(parts, 49, channels * halo)
    )
    returned = lax.all_to_all(halo_grad, "atoms", split_axis=0, concat_axis=0, tiled=True)
    returned = (
        returned.reshape(parts, 49, channels, halo)
        .transpose(1, 2, 0, 3)
        .reshape(49, channels, parts * halo)
    )
    grad_x = own_grad.at[:, :, sends].add(returned)
    summed = (
        lax.psum_scatter(grad_zero, "atoms", scatter_dimension=3, tiled=True),
        lax.psum_scatter(grad_one, "atoms", scatter_dimension=4, tiled=True),
        lax.psum_scatter(grad_two, "atoms", scatter_dimension=4, tiled=True),
    )
    factor_all = 1.0 / math.sqrt(edge_dev * parts)
    return (grad_x, summed[0] * factor_all, summed[1] * factor_all, summed[2] * factor_all)


def solution(mesh):
    in_specs = (
        P(None, "chan", "atoms"),
        P(None, "chan", "atoms"),
        P(None, "atoms"),
        P("atoms"),
        P("atoms"),
        P("atoms"),
        P("atoms"),
        P("atoms", None, None),
        P(None, "atoms"),
        P(None, "chan", None, None),
        P(None, None, "chan", None, None),
        P(None, None, "chan", None, None),
    )
    out_specs = (
        P(None, "chan", "atoms"),
        P(None, "chan", None, "atoms"),
        P(None, None, "chan", None, "atoms"),
        P(None, None, "chan", None, "atoms"),
    )
    return jax.shard_map(
        on_device, mesh=mesh, in_specs=in_specs, out_specs=out_specs, check_vma=False
    )
```

profile of v0, /device:TPU:2, one launch (start us, length us, event | category | flops | bytes accessed | tf_op | source)
XLA Modules:
  0.0 673.8 jit_solution(2438000533581852947)
XLA Ops:
  13.8 5.8 all-to-all-start.1
  20.9 3.8 gather_fusion
  24.7 5.7 copy.532
  80.5 3.3 copy.543
  167.4 4.5 gather_fusion.2
  171.9 6.8 %copy.610 = bf16[512,49,32]{0,2,1:T(8,128)(2,1)} copy(bf16[512,49,32]{1,2,0:T(8,128)(2,1)} %gather_fusion.2) | data formatting | bytes 3211264 | tf_op jit(solution)/shard_map/while/body/eval_jaxpr/gather | solution.py:149
  221.8 2.8 copy.621
  236.6 3.0 copy.619
  305.3 3.7 fusion.14
  331.0 3.6 convolution_bitcast_fusion.3
  338.5 3.5 convolution_bitcast_fusion.4
  344.8 4.5 convolution_bitcast_fusion.2
  349.2 4.0 copy.593
  353.2 4.1 convolution_bitcast_fusion.1
  357.3 3.8 copy.594
  363.7 3.2 copy.595
  373.1 3.4 copy.652
  383.2 5.4 copy.641
  395.5 9.0 %copy.596 = f32[512,49,32]{1,2,0:T(8,128)} copy(f32[512,49,32]{0,2,1:T(8,128)} %bitcast.61) | data formatting | bytes 6422528 | tf_op jit(solution)/shard_map/while/body/eval_jaxpr/concatenate | solution.py:49
  405.2 44.7 %scatter_fusion = f32[49,32,128]{0,1,2:T(8,128)S(1)} fusion(f32[49,32,128]{0,1,2:T(8,128)S(1)} %broadcast_in_dim.33, s32[512]{0:T(512)S(1)} %copy-done.55, f32[512,49,32]{1,2,0:T(8,128)} %copy.596), kind=kCustom, calls=%fused_computation.3 | custom fusion | flops 802816 | bytes 9635840 | tf_op jit(solution)/shard_map/while/body/eval_jaxpr/scatter-add | solution.py:153
  451.8 6.2 all-to-all-start
  459.3 25.3 %all-to-all-done = f32[8,49,256]{2,1,0:T(8,128)S(1)} async-done(((f32[8,49,256]{2,1,0:T(8,128)}), f32[8,49,256]{2,1,0:T(8,128)S(1)}, u32[]{:S(2)}, u32[]{:S(2)}) %all-to-all-start) | async-done | bytes 401440 | tf_op jit(solution)/shard_map/all_to_all | solution.py:171
  485.8 3.1 scatter_fusion.1
  492.5 170.4 %all-reduce.5.cloned.1.call-done = (f32[2,6,32,6,128]{2,0,3,1,4:T(2,128)}, f32[2,5,32,5,128]{2,0,3,1,4:T(2,128)}) async-done(((f32[2,6,32,6,128]{2,0,3,1,4:T(2,128)}, f32[2,5,32,5,128]{2,0,3,1,4:T(2,128)}), (f32[2,6,32,6,128]{2,0,3,1,4:T(2,128)}, f32[2,5,32,5,128]{2,0,3,1,4:T(2,128)})) %all-reduce.5.cloned.1.call-update) | async-done | bytes 1998864
  (400 shorter events, 323.8 us)
Async XLA Ops:
  7.2 12.5 %copy-start.36 = (bf16[235,512]{1,0:T(8,128)(2,1)S(1)}, bf16[235,512]{1,0:T(8,128)(2,1)}, u32[]{:S(2)}) copy-start(bf16[235,512]{1,0:T(8,128)(2,1)} %param.14) | copy-start | bytes 721924
  9.3 10.5 %copy-start.30 = (bf16[49,32,64]{2,1,0:T(8,128)(2,1)S(1)}, bf16[49,32,64]{2,1,0:T(8,128)(2,1)}, u32[]{:S(2)}) copy-start(bf16[49,32,64]{2,1,0:T(8,128)(2,1)} %param.13) | copy-start | bytes 602116
  13.8 148.9 %all-to-all-start.1 = ((bf16[8,49,256]{2,1,0:T(8,128)(2,1)}), bf16[8,49,256]{2,1,0:T(8,128)(2,1)}, u32[]{:S(2)}, u32[]{:S(2)}) async-start(bf16[8,49,256]{2,1,0:T(8,128)(2,1)} %copy.605), calls=%async_computation.1 | async-start | bytes 458752 | tf_op jit(solution)/shard_map/all_to_all | solution.py:119
  19.6 281.6 %all-gather.2.cloned.1.call-start = ((), (), s32[]{:S(2)}) async-start(), calls=%async_computation.3 | async-start | bytes 4751360 | tf_op jit(solution)/shard_map/all_gather | solution.py:144
  114.7 24.1 %copy-start.38 = (f32[1,32,512]{2,1,0:T(8,128)S(1)}, f32[1,32,512]{2,1,0:T(8,128)}, u32[]{:S(2)}) copy-start(f32[1,32,512]{2,1,0:T(8,128)} %copy.557) | copy-start | bytes 196612
  118.1 30.0 %copy-start.37 = (f32[1,32,512]{2,1,0:T(8,128)S(1)}, f32[1,32,512]{2,1,0:T(8,128)}, u32[]{:S(2)}) copy-start(f32[1,32,512]{2,1,0:T(8,128)} %copy.569) | copy-start | bytes 196612
  118.8 22.0 %copy-start.41 = (f32[1,32,512]{2,1,0:T(8,128)S(1)}, f32[1,32,512]{2,1,0:T(8,128)}, u32[]{:S(2)}) copy-start(f32[1,32,512]{2,1,0:T(8,128)} %copy.559) | copy-start | bytes 196612
  118.8 25.4 %copy-start.43 = (f32[1,32,512]{2,1,0:T(8,128)S(1)}, f32[1,32,512]{2,1,0:T(8,128)}, u32[]{:S(2)}) copy-start(f32[1,32,512]{2,1,0:T(8,128)} %copy.563) | copy-start | bytes 196612
  118.8 26.0 %copy-start.39 = (f32[1,32,512]{2,1,0:T(8,128)S(1)}, f32[1,32,512]{2,1,0:T(8,128)}, u32[]{:S(2)}) copy-start(f32[1,32,512]{2,1,0:T(8,128)} %copy.564) | copy-start | bytes 196612
  118.9 28.6 %copy-start.40 = (f32[1,32,512]{2,1,0:T(8,128)S(1)}, f32[1,32,512]{2,1,0:T(8,128)}, u32[]{:S(2)}) copy-start(f32[1,32,512]{2,1,0:T(8,128)} %copy.568) | copy-start | bytes 196612
  119.6 24.0 %copy-start.46 = (f32[1,32,512]{2,1,0:T(8,128)S(1)}, f32[1,32,512]{2,1,0:T(8,128)}, u32[]{:S(2)}) copy-start(f32[1,32,512]{2,1,0:T(8,128)} %copy.562) | copy-start | bytes 196612
  119.6 26.6 %copy-start.47 = (f32[1,32,512]{2,1,0:T(8,128)S(1)}, f32[1,32,512]{2,1,0:T(8,128)}, u32[]{:S(2)}) copy-start(f32[1,32,512]{2,1,0:T(8,128)} %copy.566) | copy-start | bytes 196612
  119.6 27.2 %copy-start.44 = (f32[1,32,512]{2,1,0:T(8,128)S(1)}, f32[1,32,512]{2,1,0:T(8,128)}, u32[]{:S(2)}) copy-start(f32[1,32,512]{2,1,0:T(8,128)} %copy.567) | copy-start | bytes 196612
  119.6 30.4 %copy-start.42 = (f32[1,32,512]{2,1,0:T(8,128)S(1)}, f32[1,32,512]{2,1,0:T(8,128)}, u32[]{:S(2)}) copy-start(f32[1,32,512]{2,1,0:T(8,128)} %copy.572) | copy-start | bytes 196612
  120.3 22.6 %copy-start.49 = (f32[1,32,512]{2,1,0:T(8,128)S(1)}, f32[1,32,512]{2,1,0:T(8,128)}, u32[]{:S(2)}) copy-start(f32[1,32,512]{2,1,0:T(8,128)} %copy.561) | copy-start | bytes 196612
  120.3 25.2 %copy-start.50 = (f32[1,32,512]{2,1,0:T(8,128)S(1)}, f32[1,32,512]{2,1,0:T(8,128)}, u32[]{:S(2)}) copy-start(f32[1,32,512]{2,1,0:T(8,128)} %copy.565) | copy-start | bytes 196612
  120.3 28.3 %copy-start.48 = (f32[1,32,512]{2,1,0:T(8,128)S(1)}, f32[1,32,512]{2,1,0:T(8,128)}, u32[]{:S(2)}) copy-start(f32[1,32,512]{2,1,0:T(8,128)} %copy.570) | copy-start | bytes 196612
  120.4 29.0 %copy-start.45 = (f32[1,32,512]{2,1,0:T(8,128)S(1)}, f32[1,32,512]{2,1,0:T(8,128)}, u32[]{:S(2)}) copy-start(f32[1,32,512]{2,1,0:T(8,128)} %copy.571) | copy-start | bytes 196612
  154.1 336.6 %reduce-scatter.2.cloned.1.call-start = ((), (), s32[]{:S(2)}) async-start(), calls=%async_computation.4 | async-start | bytes 3612672 | tf_op jit(solution)/shard_map/reduce_scatter | solution.py:179
  162.5 149.0 %copy-start.6 = (bf16[1,6,32,6,128]{4,3,2,1,0:T(8,128)(2,1)}, bf16[1,6,32,6,128]{4,3,2,1,0:T(8,128)(2,1)S(1)}, u32[]{:S(2)}) copy-start(bf16[1,6,32,6,128]{4,3,2,1,0:T(8,128)(2,1)S(1)} %copy.575) | copy-start | bytes 884740
  178.8 10.5 %copy-start.10 = (bf16[3,3,512]{1,0,2:T(4,128)(2,1)S(1)}, bf16[3,3,512]{1,0,2:T(4,128)(2,1)}, u32[]{:S(2)}) copy-start(bf16[3,3,512]{1,0,2:T(4,128)(2,1)} %copy.534) | copy-start | bytes 27652
  272.0 30.6 %copy-start.13 = (bf16[1,5,32,5,128]{4,3,2,1,0:T(8,128)(2,1)S(1)}, bf16[1,5,32,5,128]{4,3,2,1,0:T(8,128)(2,1)}, u32[]{:S(2)}) copy-start(bf16[1,5,32,5,128]{4,3,2,1,0:T(8,128)(2,1)} %copy.578) | copy-start | bytes 614404
  309.0 353.9 %all-reduce.5.cloned.1.call-start = ((), (), s32[]{:S(2)}) async-start(), calls=%async_computation.5 | async-start | bytes 15990784
  451.8 32.8 %all-to-all-start = ((f32[8,49,256]{2,1,0:T(8,128)}), f32[8,49,256]{2,1,0:T(8,128)S(1)}, u32[]{:S(2)}, u32[]{:S(2)}) async-start(f32[8,49,256]{2,1,0:T(8,128)} %copy.598), calls=%async_computation | async-start | bytes 917504 | tf_op jit(solution)/shard_map/all_to_all | solution.py:171
  (43 other events, 207.6 us)
Sparse Core Ops, SparseCore 0:
  154.2 32.4 all-gather.1
  309.1 78.1 reduce-scatter.1
  391.8 271.0 all-reduce.4
where the time goes:
time: 685 us; the launch traced here: 674 us
  local copies, waits for them, and re-layouts  318 us (46%)
  waiting for transfers between devices  196 us (29%)
  matrix products  67.4 us (10%)
  other arithmetic  63.9 us (9%)
  between operations  16.3 us (2%)
  starting transfers between devices  12.4 us (2%)
    unnamed x4, waiting for transfers between devices  170 us
    slice x68, local copies, waits for them, and re-layouts, rotate_in(): pieces[degree][min(degree, 2) + order]  91.6 us
    unnamed x188, local copies, waits for them, and re-layouts  75.9 us
    scatter-add x1, other arithmetic, one_block(): grad_table = grad_table.at[:, :, source].add(rotate_out(packed, frame_back))  44.7 us
    slice x24, local copies, waits for them, and re-layouts, rotate_in(): part_in = feature[degree * degree:degree * degree + breadth]  43.9 us
    dot_general x12, matrix products, rotate_in(): pieces.append(jnp.einsum('rke,kce->rce', matrix, part_in))  26.5 us
    all_to_all x1, waiting for transfers between devices, on_device(): lax.all_to_all(halo_grad, 'atoms', split_axis=0, concat_axis=0, tiled=True)  25.3 us
    dot_general x6, matrix products, rotate_out(): pieces.append(jnp.einsum('rke,rce->kce', matrix, stacked))  20 us
  transfers between devices with their start and end apart: 5, of which 2 were waited for; matrix products, arithmetic and copies ran while one was open for 64% of the time, Pallas kernels for 0%

commit v1 on v0

v1 whole, which is shorter than its diff:
```python
import functools
import math

import jax
import jax.numpy as jnp
from jax import lax
from jax.experimental import pallas as pl
from jax.experimental.pallas import tpu as pltpu
from jax.sharding import PartitionSpec as P

LANES = 128
BF = jnp.bfloat16
F32 = jnp.float32
VMEM_LIMIT = 56 * 1024 * 1024


def dot(a, b, dims):
    return lax.dot_general(a, b, (dims, ((), ())), preferred_element_type=F32)


NN = ((1,), (0,))
NT = ((1,), (1,))
TN = ((0,), (0,))


def degrees():
    offset = 0
    for degree in range(7):
        reach = min(degree, 2)
        yield degree, reach, offset
        offset += (2 * reach + 1) * (2 * degree + 1)


def cols(block, base=0):
    return pl.ds(pl.multiple_of(base + block * LANES, LANES), LANES)


def rotate_in(rot, raw, block, width, put):
    e = cols(block)
    for degree, reach, offset in degrees():
        breadth = 2 * degree + 1
        acc = [None] * (2 * reach + 1)
        for k in range(breadth):
            v = raw[pl.ds((degree * degree + k) * width, width), e]
            for r in range(2 * reach + 1):
                term = rot[pl.ds(offset + r * breadth + k, 1), e] * v
                acc[r] = term if acc[r] is None else acc[r] + term
        for r in range(2 * reach + 1):
            put(degree, r - reach, acc[r])


def rotate_out(rot, framed, block, width, out):
    e = cols(block)
    spots = {}
    for i, pair in enumerate(frame_pairs()):
        spots[pair] = i
    for degree, reach, offset in degrees():
        breadth = 2 * degree + 1
        u = [
            framed[pl.ds(spots[degree, m] * width, width), e]
            for m in range(-reach, reach + 1)
        ]
        for k in range(breadth):
            acc = None
            for r in range(2 * reach + 1):
                term = rot[pl.ds(offset + r * breadth + k, 1), e] * u[r]
                acc = term if acc is None else acc + term
            out[pl.ds((degree * degree + k) * width, width), e] = acc.astype(BF)


def frame_pairs():
    listing = [(degree, 0) for degree in range(7)]
    for order in (1, 2):
        listing = listing + [(degree, order) for degree in range(order, 7)]
        listing = listing + [(degree, -order) for degree in range(order, 7)]
    return listing


def onehot(ids, rows):
    return (lax.broadcasted_iota(jnp.int32, (rows, ids.shape[1]), 0) == ids).astype(BF)


def onehot_cols(ids, columns):
    return (lax.broadcasted_iota(jnp.int32, (ids.shape[0], columns), 1) == ids).astype(BF)


def prep_kernel(sends, node, cot, send_out, cot_out):
    atoms = node.shape[1]
    send_out[...] = dot(onehot_cols(sends[...], atoms), node[...], NT).astype(BF)
    eye = onehot_cols(lax.broadcasted_iota(jnp.int32, (atoms, 1), 0), atoms)
    cot_out[...] = dot(eye, cot[...], NT).astype(BF)


def frame_kernel(
    exact,
    node,
    recv,
    cot,
    rotation,
    envelope,
    source,
    target,
    count,
    valid,
    gz,
    g1,
    g2,
    *rest,
):
    if exact:
        dz_out, d1_out, d2_out, rot, raw, radial, hz, h1, h2 = rest
    else:
        d_out, rot, raw, radial, hz, h1, h2 = rest
    atoms = node.shape[1]
    slots = recv.shape[0]
    edges = rotation.shape[1]
    blocks = edges // LANES
    groups = cot.shape[0]
    width = node.shape[0] // 49
    channels = gz.shape[0] // 7
    g12 = {1: g1, 2: g2}
    h12 = {1: h1, 2: h2}

    rot[...] = rotation[...].astype(F32)
    ids = source[...]
    own = onehot(ids, atoms)
    halo = onehot(ids - atoms, slots)
    usable = jnp.sum(halo.astype(F32) * valid[...], axis=0, keepdims=True)
    usable = jnp.where(ids < atoms, 1.0, usable)
    place = lax.broadcasted_iota(jnp.int32, (1, edges), 1)
    radial[...] = jnp.where(place < count[...], envelope[...] * usable, 0.0)
    to = onehot(target[...], atoms)

    def group(q, carry):
        raw[...] = dot(cot[q], to, TN)

        def one(block, carry):
            e = cols(block)
            scale = radial[:, e]

            def put(degree, m, value):
                value = (value * scale).astype(BF)
                order = abs(m)
                row = pl.ds(
                    pl.multiple_of((degree - order) * channels + q * width, width), width
                )
                if order == 0:
                    gz[row, e] = value
                else:
                    g12[order][row, cols(block, 0 if m > 0 else edges)] = value

            rotate_in(rot, raw, block, width, put)
            return carry

        return lax.fori_loop(0, blocks, one, carry)

    lax.fori_loop(0, groups, group, 0)

    raw[...] = dot(node[...], own, NN) + dot(recv[...], halo, TN)
    hz[...] = jnp.zeros_like(hz)
    h2[...] = jnp.zeros_like(h2)

    def one_h(block, carry):
        e = cols(block)
        later = cols(block, edges)

        def put(degree, m, value):
            value = value.astype(BF)
            order = abs(m)
            first = (degree - order) * width
            second = (7 - order + degree - order) * width
            if order == 0:
                hz[pl.ds(first, width), e] = value
            elif m > 0:
                h12[order][pl.ds(first, width), e] = value
                h12[order][pl.ds(second, width), later] = value
            else:
                h12[order][pl.ds(first, width), later] = value
                h12[order][pl.ds(second, width), e] = -value

        rotate_in(rot, raw, block, width, put)
        return carry

    lax.fori_loop(0, blocks, one_h, 0)

    if exact:
        dz_out[...] = dot(gz[...], hz[...], NT)
        d1_out[...] = dot(g1[...], h1[...], NT)
        d2_out[...] = dot(g2[...], h2[...], NT)
        return
    parts = d_out.shape[0]
    share = channels // parts
    base = 0
    for count_l, g, h in ((7, gz, hz), (6, g1, h1), (5, g2, h2)):
        for degree in range(count_l):
            part = dot(g[pl.ds(degree * channels, channels), :], h[...], NT).astype(BF)
            for tile in range(h.shape[0] // LANES):
                start = base + tile * count_l * share + degree * share
                for p in range(parts):
                    d_out[p, pl.ds(start, share), :] = part[
                        p * share : (p + 1) * share, tile * LANES : (tile + 1) * LANES
                    ]
        base += h.shape[0] // LANES * count_l * share


def back_kernel(gz, g1, g2, wz, w1, w2, rotation, source, own_out, halo_out, rot, fb, y):
    edges = rotation.shape[1]
    blocks = edges // LANES
    atoms = own_out.shape[1]
    slots = halo_out.shape[0]
    width = wz.shape[0] // 7
    rot[...] = rotation[...].astype(F32)
    fb[pl.ds(0, 7 * width), :] = dot(wz[...], gz[...], NN)
    start = 7 * width
    for count_l, w, g in ((6, w1, g1), (5, w2, g2)):
        rows = count_l * width
        real = dot(w[pl.ds(0, rows), :], g[...], NN)
        imag = dot(w[pl.ds(rows, rows), :], g[...], NN)
        fb[pl.ds(start, rows), :] = real[:, :edges] + imag[:, edges:]
        fb[pl.ds(start + rows, rows), :] = real[:, edges:] - imag[:, :edges]
        start += 2 * rows

    def one(block, carry):
        rotate_out(rot, fb, block, width, y)
        return carry

    lax.fori_loop(0, blocks, one, 0)
    ids = source[...]
    own_out[...] = dot(y[...], onehot(ids, atoms), NT)
    halo_out[...] = dot(onehot(ids - atoms, slots), y[...], NT).astype(BF)


def join_kernel(own, back, sends, out):
    out[...] = own[...] + dot(back[...], onehot_cols(sends[...], own.shape[1]), TN)


def call(kernel, outs, scratch=(), flops=10**8):
    return pl.pallas_call(
        kernel,
        out_shape=outs,
        scratch_shapes=list(scratch),
        compiler_params=pltpu.CompilerParams(vmem_limit_bytes=VMEM_LIMIT),
        cost_estimate=pl.CostEstimate(
            flops=flops, bytes_accessed=8 * 10**6, transcendentals=0
        ),
    )


def on_device(
    node_x,
    cotangent,
    rotation,
    envelope,
    source,
    target,
    edge_count,
    send_index,
    halo_count,
    weight_zero,
    weight_one,
    weight_two,
):
    parts = lax.axis_size("atoms")
    groups = lax.axis_size("chan")
    width = node_x.shape[1]
    channels = width * groups
    atoms = node_x.shape[2]
    halo = send_index.shape[2]
    edges = source.shape[0]
    slots = parts * halo
    rows = 49 * width
    share = channels // parts
    exact = share % 16 != 0
    sds = jax.ShapeDtypeStruct

    node = node_x.reshape(rows, atoms)
    cot = cotangent.reshape(rows, atoms)
    sends = send_index.reshape(slots, 1)
    send_rows, cot_rows = call(
        prep_kernel, (sds((slots, rows), BF), sds((atoms, rows), BF))
    )(sends, node, cot)
    recv = lax.all_to_all(send_rows, "atoms", split_axis=0, concat_axis=0, tiled=True)
    cots = lax.all_gather(cot_rows, "chan", axis=0, tiled=False)

    valid = (
        jnp.arange(halo, dtype=jnp.int32)[None, :] < halo_count[:, 0][:, None]
    ).astype(F32).reshape(slots, 1)
    src = source.reshape(1, edges)
    tgt = target.reshape(1, edges)

    g_shapes = (
        sds((7 * channels, edges), BF),
        sds((6 * channels, 2 * edges), BF),
        sds((5 * channels, 2 * edges), BF),
    )
    pad = lambda n: -(-n // LANES) * LANES
    lz, l1, l2 = pad(7 * width), pad(12 * width), pad(10 * width)
    height = (7 * lz + 6 * l1 + 5 * l2) // LANES * share
    if exact:
        d_shapes = (
            sds((7 * channels, lz), F32),
            sds((6 * channels, l1), F32),
            sds((5 * channels, l2), F32),
        )
    else:
        d_shapes = (sds((parts, height, LANES), BF),)
    made = call(
        functools.partial(frame_kernel, exact),
        g_shapes + d_shapes,
        (
            pltpu.VMEM((235, edges), F32),
            pltpu.VMEM((rows, edges), F32),
            pltpu.VMEM((1, edges), F32),
            pltpu.VMEM((lz, edges), BF),
            pltpu.VMEM((l1, 2 * edges), BF),
            pltpu.VMEM((l2, 2 * edges), BF),
        ),
        flops=10**10,
    )(
        node,
        recv,
        cots,
        rotation,
        envelope.reshape(1, edges),
        src,
        tgt,
        edge_count.reshape(1, 1),
        valid,
    )
    gz, g1, g2 = made[:3]
    factor = 1.0 / math.sqrt(edges * parts)

    if not exact:
        pieces = lax.all_to_all(made[3], "atoms", split_axis=0, concat_axis=0, tiled=True)

    own, halo_rows = call(
        back_kernel,
        (sds((rows, atoms), F32), sds((slots, rows), BF)),
        (
            pltpu.VMEM((235, edges), F32),
            pltpu.VMEM((29 * width, edges), F32),
            pltpu.VMEM((rows, edges), BF),
        ),
        flops=10**10,
    )(
        gz,
        g1,
        g2,
        weight_zero.reshape(7 * width, 7 * channels),
        weight_one.reshape(12 * width, 6 * channels),
        weight_two.reshape(10 * width, 5 * channels),
        rotation,
        src,
    )
    back = lax.all_to_all(halo_rows, "atoms", split_axis=0, concat_axis=0, tiled=True)
    grad_x = call(join_kernel, sds((rows, atoms), F32))(own, back, sends)

    if exact:
        dz = made[3][:, : 7 * width].reshape(7, channels, 7, width)
        d1 = made[4].reshape(6, channels, 2, 6, width)
        d2 = made[5][:, : 10 * width].reshape(5, channels, 2, 5, width)
        dz = lax.psum_scatter(dz, "atoms", scatter_dimension=1, tiled=True)
        d1 = lax.psum_scatter(d1, "atoms", scatter_dimension=1, tiled=True)
        d2 = lax.psum_scatter(d2, "atoms", scatter_dimension=1, tiled=True)
    else:
        total = jnp.sum(pieces.astype(F32), axis=0)

        def take(start, count_l, lanes):
            tiles = lanes // LANES
            size = count_l * share
            got = [total[start + t * size : start + (t + 1) * size] for t in range(tiles)]
            return jnp.concatenate(got, axis=1), start + tiles * size

        dz, start = take(0, 7, lz)
        d1, start = take(start, 6, l1)
        d2, start = take(start, 5, l2)
        dz = dz[:, : 7 * width].reshape(7, share, 7, width)
        d1 = d1[:, : 12 * width].reshape(6, share, 2, 6, width)
        d2 = d2[:, : 10 * width].reshape(5, share, 2, 5, width)
    return (
        grad_x.reshape(49, width, atoms),
        dz.transpose(2, 3, 0, 1) * factor,
        d1.transpose(2, 3, 4, 0, 1) * factor,
        d2.transpose(2, 3, 4, 0, 1) * factor,
    )


def solution(mesh):
    in_specs = (
        P(None, "chan", "atoms"),
        P(None, "chan", "atoms"),
        P(None, "atoms"),
        P("atoms"),
        P("atoms"),
        P("atoms"),
        P("atoms"),
        P("atoms", None, None),
        P(None, "atoms"),
        P(None, "chan", None, None),
        P(None, None, "chan", None, None),
        P(None, None, "chan", None, None),
    )
    out_specs = (
        P(None, "chan", "atoms"),
        P(None, "chan", None, "atoms"),
        P(None, None, "chan", None, "atoms"),
        P(None, None, "chan", None, "atoms"),
    )
    return jax.shard_map(
        on_device, mesh=mesh, in_specs=in_specs, out_specs=out_specs, check_vma=False
    )
```

time: 685 us -> 108 us (0.16)
  the two profiles are of different devices: /device:TPU:2 before, /device:TPU:0 now
where the time goes in v1:
time: 108 us
  waiting for transfers between devices  33.2 us (31%)
  Pallas kernels  27.4 us (25%)
  blocking collectives  24.2 us (22%)
  starting transfers between devices  11 us (10%)
  local copies, waits for them, and re-layouts  9.29 us (9%)
  between operations  1.42 us (1%)
    all_to_all x1, waiting for transfers between devices, on_device(): lax.all_to_all(made[3], 'atoms', split_axis=0, concat_axis=0, tiled=True)  33.2 us
    pallas_call x1, Pallas kernels, on_device(): call(functools.partial(frame_kernel, exact), g_shapes + d_shapes, (pltpu....  15.6 us
    all_to_all x1, blocking collectives, on_device(): lax.all_to_all(halo_rows, 'atoms', split_axis=0, concat_axis=0, tiled=True)  14.8 us
    all_gather x1, blocking collectives, on_device(): cots = lax.all_gather(cot_rows, 'chan', axis=0, tiled=False)  9.4 us
    all_to_all x1, starting transfers between devices, on_device(): lax.all_to_all(send_rows, 'atoms', split_axis=0, concat_axis=0, tiled=True)  7.4 us
    pallas_call x1, Pallas kernels, on_device(): call(back_kernel, (sds((rows, atoms), F32), sds((slots, rows), BF)), (plt...  7.06 us
    unnamed x19, local copies, waits for them, and re-layouts  6.58 us
    all_to_all x1, starting transfers between devices, on_device(): lax.all_to_all(made[3], 'atoms', split_axis=0, concat_axis=0, tiled=True)  3.58 us
  transfers between devices with their start and end apart: 2, of which 1 were waited for; matrix products, arithmetic and copies ran while one was open for 4% of the time, Pallas kernels for 2%

profile of v1, /device:TPU:0, one launch (start us, length us, event | category | flops | bytes accessed | tf_op | source)
XLA Modules:
  0.0 107.5 jit_solution(11659116965488126920)
XLA Ops:
  0.6 1.4 %reshape.95.sends = s32[64,1]{1,0:T(8,128)} reshape(s32[1,8,8]{2,1,0:T(8,128)} %param.19) | data formatting | bytes 512 | tf_op jit(solution)/shard_map/reshape | solution.py:278
  2.1 2.3 %shard_map.147 = (bf16[64,1568]{1,0:T(8,128)(2,1)}, bf16[64,1568]{1,0:T(8,128)(2,1)}) custom-call(s32[64,1]{1,0:T(8,128)} %reshape.95.sends, bf16[1568,64]{1,0:T(8,128)(2,1)} %bitcast.44, bf16[1568,64]{1,0:T(8,128)(2,1)} %bitcast.43), custom_call_target="tpu_custom_call" | custom-call | flops 100000000 | bytes 8000000 | tf_op jit(solution)/shard_map/pallas_call | solution.py:279
  4.3 7.4 %all-to-all-start = ((bf16[8,8,1568]{2,1,0:T(8,128)(2,1)}), bf16[8,8,1568]{2,1,0:T(8,128)(2,1)S(1)}, u32[]{:S(2)}, u32[]{:S(2)}) async-start(bf16[8,8,1568]{2,1,0:T(8,128)(2,1)} %bitcast.48), calls=%async_computation | async-start | bytes 425984 | tf_op jit(solution)/shard_map/all_to_all | solution.py:282
  11.7 0.7 fusion.2
  12.5 0.7 reshape.96.valid
  13.8 0.3 copy.25
  14.1 0.9 copy.37
  15.0 0.2 copy.26
  15.2 0.8 copy.38
  16.1 0.2 copy.24
  16.2 0.8 copy.39
  17.1 9.4 %all-gather = bf16[256,1568]{1,0:T(8,128)(2,1)} all-gather(bf16[64,1568]{1,0:T(8,128)(2,1)S(1)} %copy-done.4), channel_id=2, replica_groups=mesh['atoms'=8,'chan'=4] {'chan'}, dimensions={0}, use_global_device_ids=true | all-gather | bytes 1003520 | tf_op jit(solution)/shard_map/all_gather | solution.py:283
  26.5 0.7 copy-done.3
  27.1 15.6 %shard_map.148 = (bf16[896,512]{1,0:T(8,128)(2,1)}, bf16[768,1024]{1,0:T(8,128)(2,1)}, bf16[640,1024]{1,0:T(8,128)(2,1)}, bf16[8,752,128]{2,1,0:T(8,128)(2,1)}) custom-call(bf16[1568,64]{1,0:T(8,128)(2,1)} %bitcast.45, bf16[64,1568]{1,0:T(8,128)(2,1)} %bitcast.47, bf16[4,64,1568]{2,1,0:T(8,128)(2,1)} %bitcast.39, bf16[235,512]{1,0:T(8,128)(2,1)} %rotation.3, ...), custom_call_target="tpu_custom_call" | custom-call | flops 10000000000 | bytes 8000000 | tf_op jit(solution)/shard_map/pallas_call | solution.py:307
  42.8 7.1 %shard_map.149 = (f32[1568,64]{1,0:T(8,128)}, bf16[64,1568]{1,0:T(8,128)(2,1)}) custom-call(bf16[896,512]{1,0:T(8,128)(2,1)} %get-tuple-element.14.gz, bf16[768,1024]{1,0:T(8,128)(2,1)} %get-tuple-element.15.g1, bf16[640,1024]{1,0:T(8,128)(2,1)} %get-tuple-element.16.g2, bf16[224,896]{1,0:T(8,128)(2,1)} %bitcast.46, bf16[384,768]{1,0:T(8,128)(2,1)} %bitcast.41, ...), custom_call_target="tpu_custom_call" | custom-call | flops 10000000000 | bytes 8000000 | tf_op jit(solution)/shard_map/pallas_call | solution.py:336
  49.8 14.8 %all_to_all.27 = bf16[8,8,1568]{2,1,0:T(8,128)(2,1)} all-to-all(bf16[8,8,1568]{2,1,0:T(8,128)(2,1)} %bitcast.49), channel_id=1, replica_groups=mesh['atoms'=8,'chan'=4] {'atoms'}, dimensions={0} | all-to-all | bytes 401408 | tf_op jit(solution)/shard_map/all_to_all | solution.py:355
  64.7 3.6 %all-to-all-start.2 = ((bf16[8,752,128]{2,1,0:T(8,128)(2,1)}), bf16[8,752,128]{2,1,0:T(8,128)(2,1)S(1)}, u32[]{:S(2)}, u32[]{:S(2)}) async-start(bf16[8,752,128]{2,1,0:T(8,128)(2,1)} %get-tuple-element.19), calls=%async_computation.2 | async-start | bytes 3080192 | tf_op jit(solution)/shard_map/all_to_all | solution.py:334
  68.2 2.5 %shard_map.150 = f32[1568,64]{1,0:T(8,128)} custom-call(f32[1568,64]{1,0:T(8,128)} %get-tuple-element.17.own, bf16[64,1568]{1,0:T(8,128)(2,1)} %bitcast.38, s32[64,1]{1,0:T(8,128)} %reshape.95.sends), custom_call_target="tpu_custom_call" | custom-call | flops 100000000 | bytes 8000000 | tf_op jit(solution)/shard_map/pallas_call | solution.py:356
  70.7 33.2 %all-to-all-done.2 = bf16[8,752,128]{2,1,0:T(8,128)(2,1)S(1)} async-done(((bf16[8,752,128]{2,1,0:T(8,128)(2,1)}), bf16[8,752,128]{2,1,0:T(8,128)(2,1)S(1)}, u32[]{:S(2)}, u32[]{:S(2)}) %all-to-all-start.2) | async-done | bytes 1540128 | tf_op jit(solution)/shard_map/all_to_all | solution.py:334
  103.9 0.2 convert_reduce_fusion
  104.4 0.9 copy.30
  105.3 0.2 mul.42
  105.5 1.0 copy.29
  106.7 0.8 copy.28
  (18 shorter events, 0.4 us)
Async XLA Ops:
  0.6 13.2 %copy-start = (bf16[2,6,32,6,128]{4,2,3,1,0:T(8,128)(2,1)S(1)}, bf16[2,6,32,6,128]{4,2,3,1,0:T(8,128)(2,1)}, u32[]{:S(2)}) copy-start(bf16[2,6,32,6,128]{4,2,3,1,0:T(8,128)(2,1)} %param.22) | copy-start | bytes 1769476
  4.3 10.7 %copy-start.1 = (bf16[2,5,32,5,128]{4,2,3,1,0:T(8,128)(2,1)S(1)}, bf16[2,5,32,5,128]{4,2,3,1,0:T(8,128)(2,1)}, u32[]{:S(2)}) copy-start(bf16[2,5,32,5,128]{4,2,3,1,0:T(8,128)(2,1)} %param.23) | copy-start | bytes 1228804
  4.3 22.1 %all-to-all-start = ((bf16[8,8,1568]{2,1,0:T(8,128)(2,1)}), bf16[8,8,1568]{2,1,0:T(8,128)(2,1)S(1)}, u32[]{:S(2)}, u32[]{:S(2)}) async-start(bf16[8,8,1568]{2,1,0:T(8,128)(2,1)} %bitcast.48), calls=%async_computation | async-start | bytes 425984 | tf_op jit(solution)/shard_map/all_to_all | solution.py:282
  14.1 2.0 %copy-start.2 = (bf16[7,32,7,128]{3,1,2,0:T(8,128)(2,1)S(1)}, bf16[7,32,7,128]{3,1,2,0:T(8,128)(2,1)}, u32[]{:S(2)}) copy-start(bf16[7,32,7,128]{3,1,2,0:T(8,128)(2,1)} %param.21) | copy-start | bytes 1204228
  15.2 1.8 %copy-start.4 = (bf16[64,1568]{1,0:T(8,128)(2,1)S(1)}, bf16[64,1568]{1,0:T(8,128)(2,1)}, u32[]{:S(2)}) copy-start(bf16[64,1568]{1,0:T(8,128)(2,1)} %get-tuple-element.13) | copy-start | bytes 602116
  26.5 0.7 copy-start.3
  64.7 39.3 %all-to-all-start.2 = ((bf16[8,752,128]{2,1,0:T(8,128)(2,1)}), bf16[8,752,128]{2,1,0:T(8,128)(2,1)S(1)}, u32[]{:S(2)}, u32[]{:S(2)}) async-start(bf16[8,752,128]{2,1,0:T(8,128)(2,1)} %get-tuple-element.19), calls=%async_computation.2 | async-start | bytes 3080192 | tf_op jit(solution)/shard_map/all_to_all | solution.py:334

commit v2 on v1

--- a/solution.py
+++ b/solution.py
@@ -12,6 +12,7 @@
 BF = jnp.bfloat16
 F32 = jnp.float32
 VMEM_LIMIT = 56 * 1024 * 1024
+MESH = pl.DeviceIdType.MESH
 
 
 def dot(a, b, dims):
@@ -197,7 +198,8 @@
             for tile in range(h.shape[0] // LANES):
                 start = base + tile * count_l * share + degree * share
                 for p in range(parts):
-                    d_out[p, pl.ds(start, share), :] = part[
+                    spot = (p % 2) * (parts // 2) + p // 2
+                    d_out[spot, pl.ds(start, share), :] = part[
                         p * share : (p + 1) * share, tile * LANES : (tile + 1) * LANES
                     ]
         base += h.shape[0] // LANES * count_l * share
@@ -234,12 +236,265 @@
     out[...] = own[...] + dot(back[...], onehot_cols(sends[...], own.shape[1]), TN)
 
 
-def call(kernel, outs, scratch=(), flops=10**8):
+def exchange_kernel(
+    sends,
+    node,
+    cot,
+    recv_out,
+    cot_out,
+    mine,
+    land,
+    cots,
+    halo_sent,
+    halo_got,
+    chan_sent,
+    chan_got,
+):
+    parts, halo, _ = land.shape
+    groups = cots.shape[0]
+    atoms = node.shape[1]
+    me = lax.axis_index("atoms")
+    group = lax.axis_index("chan")
+    barrier = pltpu.get_barrier_semaphore()
+    for k in range(1, parts):
+        pl.semaphore_signal(
+            barrier, inc=1, device_id={"atoms": lax.rem(me + k, parts)}, device_id_type=MESH
+        )
+    for k in range(1, groups):
+        pl.semaphore_signal(
+            barrier, inc=1, device_id={"chan": lax.rem(group + k, groups)}, device_id_type=MESH
+        )
+    eye = onehot_cols(lax.broadcasted_iota(jnp.int32, (atoms, 1), 0), atoms)
+    cots[group] = dot(eye, cot[...], NT).astype(BF)
+    picked = dot(onehot_cols(sends[...], atoms), node[...], NT).astype(BF)
+    for p in range(parts):
+        mine[p] = picked[p * halo : (p + 1) * halo, :]
+    pl.semaphore_wait(barrier, parts + groups - 2)
+    copies = []
+    for k in range(1, parts):
+        peer = lax.rem(me + k, parts)
+        copies.append(
+            pltpu.make_async_remote_copy(
+                src_ref=mine.at[peer],
+                dst_ref=land.at[me],
+                send_sem=halo_sent.at[k],
+                recv_sem=halo_got.at[k],
+                device_id={"atoms": peer},
+                device_id_type=MESH,
+            )
+        )
+    for k in range(1, groups):
+        peer = lax.rem(group + k, groups)
+        copies.append(
+            pltpu.make_async_remote_copy(
+                src_ref=cots.at[group],
+                dst_ref=cots.at[group],
+                send_sem=chan_sent.at[k],
+                recv_sem=chan_got.at[k],
+                device_id={"chan": peer},
+                device_id_type=MESH,
+            )
+        )
+    for copy in copies:
+        copy.start()
+    land[me] = mine[me]
+    for copy in copies:
+        copy.wait()
+    recv_out[...] = land[...]
+    cot_out[...] = cots[...]
+
+
+def finish_kernel(
+    factor,
+    gz,
+    g1,
+    g2,
+    wz_in,
+    w1_in,
+    w2_in,
+    rotation,
+    source,
+    sends,
+    pieces,
+    x_out,
+    dz_out,
+    d1_out,
+    d2_out,
+    wz,
+    w1,
+    w2,
+    rot,
+    fb,
+    y,
+    halo_mine,
+    halo_land,
+    near,
+    passing,
+    far,
+    total,
+    near_sent,
+    near_got,
+    far_sent,
+    far_got,
+    halo_sent,
+    halo_got,
+):
+    edges = rotation.shape[1]
+    blocks = edges // LANES
+    atoms = x_out.shape[1]
+    parts, halo, rows_x = halo_land.shape
+    slots = parts * halo
+    width = wz.shape[0] // 7
+    channels = wz.shape[1] // 7
+    share = channels // parts
+    half = parts // 2
+    me = lax.axis_index("atoms")
+    line, side = me // 2, lax.rem(me, 2)
+    other = line * 2 + 1 - side
+
+    barrier = pltpu.get_barrier_semaphore()
+    for k in range(1, parts):
+        pl.semaphore_signal(
+            barrier, inc=1, device_id={"atoms": lax.rem(me + k, parts)}, device_id_type=MESH
+        )
+    rot[...] = rotation[...].astype(F32)
+    for i in range(7):
+        for j in range(7):
+            wz[i * width : (i + 1) * width, j * channels : (j + 1) * channels] = wz_in[i, j]
+    for count_l, w, w_in in ((6, w1, w1_in), (5, w2, w2_in)):
+        for part in range(2):
+            for i in range(count_l):
+                for j in range(count_l):
+                    at = (part * count_l + i) * width
+                    w[at : at + width, j * channels : (j + 1) * channels] = w_in[part, i, j]
+    pl.semaphore_wait(barrier, parts - 1)
+
+    lanes = ((7, dz_out), (6, d1_out), (5, d2_out))
+    tiles = [-(-(count_l if i == 0 else 2 * count_l) * width // LANES) for i, (count_l, _) in enumerate(lanes)]
+    chunks = []
+    start = 0
+    for (count_l, _), t in zip(lanes, tiles):
+        size = t * count_l * share
+        chunks.append((start, size))
+        start += size
+
+    near_copies = []
+    for c, (start, size) in enumerate(chunks):
+        copy = pltpu.make_async_remote_copy(
+            src_ref=pieces.at[pl.ds((1 - side) * half, half), pl.ds(start, size), :],
+            dst_ref=near.at[:, pl.ds(start, size), :],
+            send_sem=near_sent.at[c],
+            recv_sem=near_got.at[c],
+            device_id={"atoms": other},
+            device_id_type=MESH,
+        )
+        copy.start()
+        near_copies.append(copy)
+
+    far_copies = []
+
+    def pass_on(c):
+        start, size = chunks[c]
+        near_copies[c].wait_recv()
+        window = pl.ds(start, size)
+        for k in range(half):
+            place = lax.rem(line + k, half)
+            value = pieces[side * half + place, window, :].astype(F32) + near[
+                place, window, :
+            ].astype(F32)
+            if k == 0:
+                total[window, :] = value
+                continue
+            passing[k - 1, window, :] = value.astype(BF)
+            copy = pltpu.make_async_remote_copy(
+                src_ref=passing.at[k - 1, window, :],
+                dst_ref=far.at[k - 1, window, :],
+                send_sem=far_sent.at[c, k - 1],
+                recv_sem=far_got.at[c, k - 1],
+                device_id={"atoms": place * 2 + side},
+                device_id_type=MESH,
+            )
+            copy.start()
+            far_copies.append((c, copy))
+
+    fb[pl.ds(0, 7 * width), :] = dot(wz[...], gz[...], NN)
+    start = 7 * width
+    for count_l, w, g in ((6, w1, g1), (5, w2, g2)):
+        rows = count_l * width
+        real = dot(w[pl.ds(0, rows), :], g[...], NN)
+        imag = dot(w[pl.ds(rows, rows), :], g[...], NN)
+        fb[pl.ds(start, rows), :] = real[:, :edges] + imag[:, edges:]
+        fb[pl.ds(start + rows, rows), :] = real[:, edges:] - imag[:, :edges]
+        start += 2 * rows
+
+    def one(block, carry):
+        rotate_out(rot, fb, block, width, y)
+        return carry
+
+    lax.fori_loop(0, blocks, one, 0)
+    ids = source[...]
+    halo_terms = dot(onehot(ids - atoms, slots), y[...], NT).astype(BF)
+    for p in range(parts):
+        halo_mine[p] = halo_terms[p * halo : (p + 1) * halo, :]
+    halo_copies = []
+    for k in range(1, parts):
+        peer = lax.rem(me + k, parts)
+        copy = pltpu.make_async_remote_copy(
+            src_ref=halo_mine.at[peer],
+            dst_ref=halo_land.at[me],
+            send_sem=halo_sent.at[k],
+            recv_sem=halo_got.at[k],
+            device_id={"atoms": peer},
+            device_id_type=MESH,
+        )
+        copy.start()
+        halo_copies.append(copy)
+    halo_land[me] = halo_mine[me]
+    pass_on(0)
+    x_out[...] = dot(y[...], onehot(ids, atoms), NT)
+    pass_on(1)
+    for copy in halo_copies:
+        copy.wait_recv()
+    back = halo_land[...].astype(F32).reshape(slots, rows_x).astype(BF)
+    x_out[...] += dot(back, onehot_cols(sends[...], atoms), TN)
+    pass_on(2)
+
+    for c, (count_l, out) in enumerate(lanes):
+        start, size = chunks[c]
+        window = pl.ds(start, size)
+        value = total[window, :]
+        for at, copy in far_copies:
+            if at == c:
+                copy.wait_recv()
+        for k in range(half - 1):
+            value = value + far[k, window, :].astype(F32)
+        value = value * factor
+        for i in range(count_l if c == 0 else 2 * count_l):
+            tile, lane = divmod(i * width, LANES)
+            for j in range(count_l):
+                row = (tile * count_l + j) * share
+                cut = value[row : row + share, lane : lane + width]
+                if c == 0:
+                    out[i, j] = cut
+                else:
+                    out[i // count_l, i % count_l, j] = cut
+
+    for copy in near_copies + halo_copies + [copy for _, copy in far_copies]:
+        copy.wait_send()
+
+
+def call(kernel, outs, scratch=(), flops=10**8, collective=None):
+    if collective is None:
+        params = pltpu.CompilerParams(vmem_limit_bytes=VMEM_LIMIT)
+    else:
+        params = pltpu.CompilerParams(
+            vmem_limit_bytes=VMEM_LIMIT, collective_id=collective, has_side_effects=True
+        )
     return pl.pallas_call(
         kernel,
         out_shape=outs,
         scratch_shapes=list(scratch),
-        compiler_params=pltpu.CompilerParams(vmem_limit_bytes=VMEM_LIMIT),
+        compiler_params=params,
         cost_estimate=pl.CostEstimate(
             flops=flops, bytes_accessed=8 * 10**6, transcendentals=0
         ),
@@ -270,17 +525,35 @@
     slots = parts * halo
     rows = 49 * width
     share = channels // parts
-    exact = share % 16 != 0
+    exact = parts != 8 or share % 16 != 0
     sds = jax.ShapeDtypeStruct
 
     node = node_x.reshape(rows, atoms)
     cot = cotangent.reshape(rows, atoms)
     sends = send_index.reshape(slots, 1)
-    send_rows, cot_rows = call(
-        prep_kernel, (sds((slots, rows), BF), sds((atoms, rows), BF))
-    )(sends, node, cot)
-    recv = lax.all_to_all(send_rows, "atoms", split_axis=0, concat_axis=0, tiled=True)
-    cots = lax.all_gather(cot_rows, "chan", axis=0, tiled=False)
+    dma = pltpu.SemaphoreType.DMA
+    if exact:
+        send_rows, cot_rows = call(
+            prep_kernel, (sds((slots, rows), BF), sds((atoms, rows), BF))
+        )(sends, node, cot)
+        recv = lax.all_to_all(send_rows, "atoms", split_axis=0, concat_axis=0, tiled=True)
+        cots = lax.all_gather(cot_rows, "chan", axis=0, tiled=False)
+    else:
+        recv, cots = call(
+            exchange_kernel,
+            (sds((parts, halo, rows), BF), sds((groups, atoms, rows), BF)),
+            (
+                pltpu.VMEM((parts, halo, rows), BF),
+                pltpu.VMEM((parts, halo, rows), BF),
+                pltpu.VMEM((groups, atoms, rows), BF),
+                dma((parts,)),
+                dma((parts,)),
+                dma((groups,)),
+                dma((groups,)),
+            ),
+            collective=0,
+        )(sends, node, cot)
+        recv = recv.reshape(slots, rows)
 
     valid = (
         jnp.arange(halo, dtype=jnp.int32)[None, :] < halo_count[:, 0][:, None]
@@ -331,7 +604,55 @@
     factor = 1.0 / math.sqrt(edges * parts)
 
     if not exact:
-        pieces = lax.all_to_all(made[3], "atoms", split_axis=0, concat_axis=0, tiled=True)
+        half = parts // 2
+        grad_x, dz, d1, d2 = call(
+            functools.partial(finish_kernel, factor),
+            (
+                sds((rows, atoms), F32),
+                sds((7, 7, share, width), F32),
+                sds((2, 6, 6, share, width), F32),
+                sds((2, 5, 5, share, width), F32),
+            ),
+            (
+                pltpu.VMEM((7 * width, 7 * channels), BF),
+                pltpu.VMEM((12 * width, 6 * channels), BF),
+                pltpu.VMEM((10 * width, 5 * channels), BF),
+                pltpu.VMEM((235, edges), F32),
+                pltpu.VMEM((29 * width, edges), F32),
+                pltpu.VMEM((rows, edges), BF),
+                pltpu.VMEM((parts, halo, rows), BF),
+                pltpu.VMEM((parts, halo, rows), BF),
+                pltpu.VMEM((half, height, LANES), BF),
+                pltpu.VMEM((half - 1, height, LANES), BF),
+                pltpu.VMEM((half - 1, height, LANES), BF),
+                pltpu.VMEM((height, LANES), F32),
+                dma((3,)),
+                dma((3,)),
+                dma((3, half - 1)),
+                dma((3, half - 1)),
+                dma((parts,)),
+                dma((parts,)),
+            ),
+            flops=10**10,
+            collective=1,
+        )(
+            gz,
+            g1,
+            g2,
+            weight_zero.transpose(0, 2, 1, 3),
+            weight_one.transpose(0, 1, 3, 2, 4),
+            weight_two.transpose(0, 1, 3, 2, 4),
+            rotation,
+            src,
+            sends,
+            made[3],
+        )
+        return (
+            grad_x.reshape(49, width, atoms),
+            dz.transpose(0, 3, 1, 2),
+            d1.transpose(0, 1, 4, 2, 3),
+            d2.transpose(0, 1, 4, 2, 3),
+        )
 
     own, halo_rows = call(
         back_kernel,
@@ -355,28 +676,12 @@
     back = lax.all_to_all(halo_rows, "atoms", split_axis=0, concat_axis=0, tiled=True)
     grad_x = call(join_kernel, sds((rows, atoms), F32))(own, back, sends)
 
-    if exact:
-        dz = made[3][:, : 7 * width].reshape(7, channels, 7, width)
-        d1 = made[4].reshape(6, channels, 2, 6, width)
-        d2 = made[5][:, : 10 * width].reshape(5, channels, 2, 5, width)
-        dz = lax.psum_scatter(dz, "atoms", scatter_dimension=1, tiled=True)
-        d1 = lax.psum_scatter(d1, "atoms", scatter_dimension=1, tiled=True)
-        d2 = lax.psum_scatter(d2, "atoms", scatter_dimension=1, tiled=True)
-    else:
-        total = jnp.sum(pieces.astype(F32), axis=0)
-
-        def take(start, count_l, lanes):
-            tiles = lanes // LANES
-            size = count_l * share
-            got = [total[start + t * size : start + (t + 1) * size] for t in range(tiles)]
-            return jnp.concatenate(got, axis=1), start + tiles * size
-
-        dz, start = take(0, 7, lz)
-        d1, start = take(start, 6, l1)
-        d2, start = take(start, 5, l2)
-        dz = dz[:, : 7 * width].reshape(7, share, 7, width)
-        d1 = d1[:, : 12 * width].reshape(6, share, 2, 6, width)
-        d2 = d2[:, : 10 * width].reshape(5, share, 2, 5, width)
+    dz = made[3][:, : 7 * width].reshape(7, channels, 7, width)
+    d1 = made[4].reshape(6, channels, 2, 6, width)
+    d2 = made[5][:, : 10 * width].reshape(5, channels, 2, 5, width)
+    dz = lax.psum_scatter(dz, "atoms", scatter_dimension=1, tiled=True)
+    d1 = lax.psum_scatter(d1, "atoms", scatter_dimension=1, tiled=True)
+    d2 = lax.psum_scatter(d2, "atoms", scatter_dimension=1, tiled=True)
     return (
         grad_x.reshape(49, width, atoms),
         dz.transpose(2, 3, 0, 1) * factor,

time: 108 us -> 76.9 us (0.71)
  the two profiles are of different devices: /device:TPU:0 before, /device:TPU:2 now
where the time goes in v2:
time: 76.9 us; the launch traced here: 75.8 us
  Pallas kernels  67.1 us (87%)
  local copies, waits for them, and re-layouts  6.58 us (9%)
  between operations  1.32 us (2%)
    pallas_call x1, Pallas kernels, on_device(): call(functools.partial(finish_kernel, factor), (sds((rows, atoms), F32),...  35.5 us
    pallas_call x1, Pallas kernels, on_device(): call(exchange_kernel, (sds((parts, halo, rows), BF), sds((groups, atoms,...  16 us
    pallas_call x1, Pallas kernels, on_device(): call(functools.partial(frame_kernel, exact), g_shapes + d_shapes, (pltpu....  15.6 us
    unnamed x10, local copies, waits for them, and re-layouts  4.51 us

profile of v2, /device:TPU:2, one launch (start us, length us, event | category | flops | bytes accessed | tf_op | source)
XLA Modules:
  0.0 75.8 jit_solution(3926611603365936111)
XLA Ops:
  1.3 0.7 fusion
  2.0 0.7 reshape.74.valid
  2.7 1.4 %reshape.73.sends = s32[64,1]{1,0:T(8,128)} reshape(s32[1,8,8]{2,1,0:T(8,128)} %param.19) | data formatting | bytes 512 | tf_op jit(solution)/shard_map/reshape | solution.py:533
  4.1 16.0 %shard_map.147 = (bf16[8,8,1568]{2,1,0:T(8,128)(2,1)}, bf16[4,64,1568]{2,1,0:T(8,128)(2,1)}) custom-call(s32[64,1]{1,0:T(8,128)} %reshape.73.sends, bf16[1568,64]{1,0:T(8,128)(2,1)} %bitcast.20, bf16[1568,64]{1,0:T(8,128)(2,1)} %bitcast.19), custom_call_target="tpu_custom_call" | custom-call | flops 100000000 | bytes 8000000 | tf_op jit(solution)/shard_map/pallas_call | solution.py:542
  20.1 15.6 %shard_map.148 = (bf16[896,512]{1,0:T(8,128)(2,1)}, bf16[768,1024]{1,0:T(8,128)(2,1)}, bf16[640,1024]{1,0:T(8,128)(2,1)}, bf16[8,752,128]{2,1,0:T(8,128)(2,1)}) custom-call(bf16[1568,64]{1,0:T(8,128)(2,1)} %bitcast.21, bf16[64,1568]{1,0:T(8,128)(2,1)} %bitcast.27, bf16[4,64,1568]{2,1,0:T(8,128)(2,1)} %get-tuple-element.15.cot, bf16[235,512]{1,0:T(8,128)(2,1)} %rotation.3, ...), custom_call_target="tpu_custom_call" | custom-call | flops 10000000000 | bytes 8000000 | tf_op jit(solution)/shard_map/pallas_call | solution.py:580
  35.8 35.5 %shard_map.149 = (f32[1568,64]{1,0:T(8,128)}, f32[7,7,16,32]{3,2,1,0:T(8,128)}, f32[2,6,6,16,32]{4,3,2,1,0:T(8,128)}, f32[2,5,5,16,32]{4,3,2,1,0:T(8,128)}) custom-call(bf16[896,512]{1,0:T(8,128)(2,1)} %get-tuple-element.16.gz, bf16[768,1024]{1,0:T(8,128)(2,1)} %get-tuple-element.17.g1, bf16[640,1024]{1,0:T(8,128)(2,1)} %get-tuple-element.18.g2, ...), custom_call_target="tpu_custom_call" | custom-call | flops 10000000000 | bytes 8000000 | tf_op jit(solution)/shard_map/pallas_call | solution.py:608
  71.2 0.0 copy-start.2
  71.2 0.0 copy-start
  71.2 0.0 copy-start.1
  71.2 2.2 %copy.24 = f32[49,32,64]{2,1,0:T(8,128)} copy(f32[49,32,64]{2,1,0:T(8,128)} %bitcast.16) | data formatting | bytes 802816
  73.4 0.0 copy-done.2
  73.4 0.7 copy.25
  74.2 0.0 copy-done
  74.2 0.8 %copy.26 = f32[2,6,32,6,16]{2,4,3,1,0:T(8,128)} copy(f32[2,6,32,6,16]{2,4,3,1,0:T(8,128)S(1)} %bitcast.17) | data formatting | bytes 294912
  75.0 0.0 copy-done.1
  75.0 0.8 copy.27
Async XLA Ops:
  71.2 2.2 %copy-start.2 = (f32[7,7,16,32]{3,2,1,0:T(8,128)S(1)}, f32[7,7,16,32]{3,2,1,0:T(8,128)}, u32[]{:S(2)}) copy-start(f32[7,7,16,32]{3,2,1,0:T(8,128)} %get-tuple-element.21) | copy-start | bytes 301060
  71.2 3.0 %copy-start = (f32[2,6,6,16,32]{4,3,2,1,0:T(8,128)S(1)}, f32[2,6,6,16,32]{4,3,2,1,0:T(8,128)}, u32[]{:S(2)}) copy-start(f32[2,6,6,16,32]{4,3,2,1,0:T(8,128)} %get-tuple-element.22) | copy-start | bytes 442372
  71.2 3.8 %copy-start.1 = (f32[2,5,5,16,32]{4,3,2,1,0:T(8,128)S(1)}, f32[2,5,5,16,32]{4,3,2,1,0:T(8,128)}, u32[]{:S(2)}) copy-start(f32[2,5,5,16,32]{4,3,2,1,0:T(8,128)} %get-tuple-element.23) | copy-start | bytes 307204

commit v3 on v1

--- a/solution.py
+++ b/solution.py
@@ -12,6 +12,7 @@
 BF = jnp.bfloat16
 F32 = jnp.float32
 VMEM_LIMIT = 56 * 1024 * 1024
+MESH = pl.DeviceIdType.MESH
 
 
 def dot(a, b, dims):
@@ -92,7 +93,6 @@
 
 
 def frame_kernel(
-    exact,
     node,
     recv,
     cot,
@@ -105,12 +105,16 @@
     gz,
     g1,
     g2,
-    *rest,
+    dz_out,
+    d1_out,
+    d2_out,
+    rot,
+    raw,
+    radial,
+    hz,
+    h1,
+    h2,
 ):
-    if exact:
-        dz_out, d1_out, d2_out, rot, raw, radial, hz, h1, h2 = rest
-    else:
-        d_out, rot, raw, radial, hz, h1, h2 = rest
     atoms = node.shape[1]
     slots = recv.shape[0]
     edges = rotation.shape[1]
@@ -183,24 +187,9 @@
 
     lax.fori_loop(0, blocks, one_h, 0)
 
-    if exact:
-        dz_out[...] = dot(gz[...], hz[...], NT)
-        d1_out[...] = dot(g1[...], h1[...], NT)
-        d2_out[...] = dot(g2[...], h2[...], NT)
-        return
-    parts = d_out.shape[0]
-    share = channels // parts
-    base = 0
-    for count_l, g, h in ((7, gz, hz), (6, g1, h1), (5, g2, h2)):
-        for degree in range(count_l):
-            part = dot(g[pl.ds(degree * channels, channels), :], h[...], NT).astype(BF)
-            for tile in range(h.shape[0] // LANES):
-                start = base + tile * count_l * share + degree * share
-                for p in range(parts):
-                    d_out[p, pl.ds(start, share), :] = part[
-                        p * share : (p + 1) * share, tile * LANES : (tile + 1) * LANES
-                    ]
-        base += h.shape[0] // LANES * count_l * share
+    dz_out[...] = dot(gz[...], hz[...], NT)
+    d1_out[...] = dot(g1[...], h1[...], NT)
+    d2_out[...] = dot(g2[...], h2[...], NT)
 
 
 def back_kernel(gz, g1, g2, wz, w1, w2, rotation, source, own_out, halo_out, rot, fb, y):
@@ -234,12 +223,354 @@
     out[...] = own[...] + dot(back[...], onehot_cols(sends[...], own.shape[1]), TN)
 
 
-def call(kernel, outs, scratch=(), flops=10**8):
+def column(row):
+    n = row.shape[1]
+    diag = lax.broadcasted_iota(jnp.int32, (n, n), 0) == lax.broadcasted_iota(
+        jnp.int32, (n, n), 1
+    )
+    spread = jnp.where(diag, jnp.broadcast_to(row.astype(F32), (n, n)), 0.0)
+    return jnp.sum(spread, axis=1, keepdims=True)
+
+
+def whole_kernel(
+    factor,
+    sends_in,
+    node,
+    cot,
+    rotation,
+    envelope,
+    source,
+    target,
+    count,
+    counts_in,
+    wz_in,
+    w1_in,
+    w2_in,
+    x_out,
+    dz_out,
+    d1_out,
+    d2_out,
+    mine,
+    land,
+    cots,
+    rot,
+    raw,
+    radial,
+    gz,
+    g1,
+    g2,
+    qz,
+    q1,
+    q2,
+    hz,
+    h1,
+    h2,
+    wz,
+    w1,
+    w2,
+    fb,
+    y,
+    back_mine,
+    back_land,
+    pieces,
+    near,
+    passing,
+    far,
+    total,
+    halo_sent,
+    halo_got,
+    chan_sent,
+    chan_got,
+    near_sent,
+    near_got,
+    far_sent,
+    far_got,
+    back_sent,
+    back_got,
+):
+    parts, halo, rows_x = land.shape
+    groups = cots.shape[0]
+    atoms = node.shape[1]
+    slots = parts * halo
+    edges = rotation.shape[1]
+    blocks = edges // LANES
+    width = rows_x // 49
+    channels = width * groups
+    share = channels // parts
+    me = lax.axis_index("atoms")
+    group = lax.axis_index("chan")
+    line, side = me // 2, lax.rem(me, 2)
+    other = line * 2 + 1 - side
+
+    def push(src, dst, sent, got, where):
+        return pltpu.make_async_remote_copy(
+            src_ref=src,
+            dst_ref=dst,
+            send_sem=sent,
+            recv_sem=got,
+            device_id=where,
+            device_id_type=MESH,
+        )
+
+    barrier = pltpu.get_barrier_semaphore()
+    for k in range(1, parts):
+        pl.semaphore_signal(
+            barrier, inc=1, device_id={"atoms": lax.rem(me + k, parts)}, device_id_type=MESH
+        )
+    for k in range(1, groups):
+        pl.semaphore_signal(
+            barrier, inc=1, device_id={"chan": lax.rem(group + k, groups)}, device_id_type=MESH
+        )
+    sends = jnp.concatenate([column(sends_in[p : p + 1, :]) for p in range(parts)], axis=0)
+    sends = sends.astype(jnp.int32)
+    eye = onehot_cols(lax.broadcasted_iota(jnp.int32, (atoms, 1), 0), atoms)
+    cots[group] = dot(eye, cot[...], NT).astype(BF)
+    picked = dot(onehot_cols(sends, atoms), node[...], NT).astype(BF)
+    for p in range(parts):
+        mine[p] = picked[p * halo : (p + 1) * halo, :]
+    pl.semaphore_wait(barrier, parts + groups - 2)
+
+    halo_copies = []
+    for k in range(1, parts):
+        peer = lax.rem(me + k, parts)
+        copy = push(
+            mine.at[peer], land.at[me], halo_sent.at[k], halo_got.at[k], {"atoms": peer}
+        )
+        copy.start()
+        halo_copies.append(copy)
+    chan_copies = []
+    for k in range(1, groups):
+        peer = lax.rem(group + k, groups)
+        copy = push(
+            cots.at[group], cots.at[group], chan_sent.at[k], chan_got.at[k], {"chan": peer}
+        )
+        copy.start()
+        chan_copies.append(copy)
+    land[me] = mine[me]
+
+    rot[...] = rotation[...].astype(F32)
+    ids = source[...]
+    own = onehot(ids, atoms)
+    remote = onehot(ids - atoms, slots)
+    order = lax.broadcasted_iota(jnp.int32, (halo, 1), 0)
+    valid = jnp.concatenate(
+        [(order < counts_in[:, p : p + 1]).astype(F32) for p in range(parts)], axis=0
+    )
+    usable = jnp.sum(remote.astype(F32) * valid, axis=0, keepdims=True)
+    usable = jnp.where(ids < atoms, 1.0, usable)
+    place = lax.broadcasted_iota(jnp.int32, (1, edges), 1)
+    radial[...] = jnp.where(place < count[...], envelope[...] * usable, 0.0)
+    to = onehot(target[...], atoms)
+
+    g12 = {1: g1, 2: g2}
+    q12 = {1: q1, 2: q2}
+    h12 = {1: h1, 2: h2}
+
+    def frame_grad(q):
+        raw[...] = dot(cots[q], to, TN)
+
+        def one(block, carry):
+            e = cols(block)
+            scale = radial[:, e]
+
+            def put(degree, m, value):
+                value = (value * scale).astype(BF)
+                o = abs(m)
+                row = pl.ds(
+                    pl.multiple_of((degree - o) * channels + q * width, width), width
+                )
+                short = pl.ds((degree - o) * width, width)
+                if o == 0:
+                    gz[row, e] = value
+                    qz[short, e] = value
+                else:
+                    at = cols(block, 0 if m > 0 else edges)
+                    g12[o][row, at] = value
+                    q12[o][short, at] = value
+
+            rotate_in(rot, raw, block, width, put)
+            return carry
+
+        lax.fori_loop(0, blocks, one, 0)
+
+    def one_h(block, carry):
+        e = cols(block)
+        later = cols(block, edges)
+
+        def put(degree, m, value):
+            value = value.astype(BF)
+            o = abs(m)
+            first = (degree - o) * width
+            second = (7 - o + degree - o) * width
+            if o == 0:
+                hz[pl.ds(first, width), e] = value
+            elif m > 0:
+                h12[o][pl.ds(first, width), e] = value
+                h12[o][pl.ds(second, width), later] = value
+            else:
+                h12[o][pl.ds(first, width), later] = value
+                h12[o][pl.ds(second, width), e] = -value
+
+        rotate_in(rot, raw, block, width, put)
+        return carry
+
+    near_copies = []
+
+    def weight_piece(k):
+        base = 0
+        for count_l, g, h in ((7, qz, hz), (6, q1, h1), (5, q2, h2)):
+            part = dot(g[...], h[...], NT).astype(BF)
+            tiles = h.shape[0] // LANES
+            for tile in range(tiles):
+                for degree in range(count_l):
+                    start = base + (tile * count_l + degree) * share
+                    for half in range(2):
+                        row = degree * width + half * share
+                        pieces[k, half, start : start + share, :] = part[
+                            row : row + share, tile * LANES : (tile + 1) * LANES
+                        ]
+            base += tiles * count_l * share
+        copy = push(
+            pieces.at[k, 1 - side],
+            near.at[k],
+            near_sent.at[k],
+            near_got.at[k],
+            {"atoms": other},
+        )
+        copy.start()
+        near_copies.append(copy)
+
+    def far_copy(k, q):
+        slot = lax.rem(line - q + groups + groups - 1, groups)
+        return push(
+            passing.at[k],
+            far.at[slot],
+            far_sent.at[k],
+            far_got.at[slot],
+            {"atoms": q * 2 + side},
+        )
+
+    def pass_on(k):
+        near_copies[k].wait_recv()
+        q = lax.rem(group + k, groups)
+        value = pieces[k, side].astype(F32) + near[k].astype(F32)
+
+        @pl.when(q == line)
+        def keep():
+            total[...] = value
+
+        @pl.when(q != line)
+        def send():
+            passing[k] = value.astype(BF)
+            far_copy(k, q).start()
+
+    frame_grad(group)
+    for copy in halo_copies:
+        copy.wait_recv()
+    hz[...] = jnp.zeros_like(hz)
+    h2[...] = jnp.zeros_like(h2)
+    table = land[...].astype(F32).reshape(slots, rows_x).astype(BF)
+    raw[...] = dot(node[...], own, NN) + dot(table, remote, TN)
+    lax.fori_loop(0, blocks, one_h, 0)
+    weight_piece(0)
+
+    for i in range(7):
+        for j in range(7):
+            wz[i * width : (i + 1) * width, j * channels : (j + 1) * channels] = wz_in[i, j]
+    for count_l, w, w_in in ((6, w1, w1_in), (5, w2, w2_in)):
+        for part in range(2):
+            for i in range(count_l):
+                for j in range(count_l):
+                    at = (part * count_l + i) * width
+                    w[at : at + width, j * channels : (j + 1) * channels] = w_in[part, i, j]
+
+    for k in range(1, groups):
+        chan_copies[groups - k - 1].wait_recv()
+        frame_grad(lax.rem(group + k, groups))
+        weight_piece(k)
+        pass_on(k - 1)
+
+    fb[pl.ds(0, 7 * width), :] = dot(wz[...], gz[...], NN)
+    start = 7 * width
+    for count_l, w, g in ((6, w1, g1), (5, w2, g2)):
+        rows = count_l * width
+        real = dot(w[pl.ds(0, rows), :], g[...], NN)
+        imag = dot(w[pl.ds(rows, rows), :], g[...], NN)
+        fb[pl.ds(start, rows), :] = real[:, :edges] + imag[:, edges:]
+        fb[pl.ds(start + rows, rows), :] = real[:, edges:] - imag[:, :edges]
+        start += 2 * rows
+    pass_on(groups - 1)
+
+    def one_back(block, carry):
+        rotate_out(rot, fb, block, width, y)
+        return carry
+
+    lax.fori_loop(0, blocks, one_back, 0)
+    terms = dot(remote, y[...], NT).astype(BF)
+    for p in range(parts):
+        back_mine[p] = terms[p * halo : (p + 1) * halo, :]
+    back_copies = []
+    for k in range(1, parts):
+        peer = lax.rem(me + k, parts)
+        copy = push(
+            back_mine.at[peer],
+            back_land.at[me],
+            back_sent.at[k],
+            back_got.at[k],
+            {"atoms": peer},
+        )
+        copy.start()
+        back_copies.append(copy)
+    back_land[me] = back_mine[me]
+    x_out[...] = dot(y[...], own, NT)
+
+    value = total[...]
+    for j in range(groups - 1):
+        push(
+            passing.at[0], far.at[j], far_sent.at[0], far_got.at[j], {"atoms": other}
+        ).wait_recv()
+        value = value + far[j].astype(F32)
+    total[...] = value * factor
+    base = 0
+    for c, (count_l, h, out) in enumerate(((7, hz, dz_out), (6, h1, d1_out), (5, h2, d2_out))):
+        for i in range(count_l if c == 0 else 2 * count_l):
+            tile, lane = divmod(i * width, LANES)
+            for j in range(count_l):
+                row = base + (tile * count_l + j) * share
+                cut = total[row : row + share, lane : lane + width]
+                if c == 0:
+                    out[i, j] = cut
+                else:
+                    out[i // count_l, i % count_l, j] = cut
+        base += h.shape[0] // LANES * count_l * share
+
+    for copy in back_copies:
+        copy.wait_recv()
+    returned = back_land[...].astype(F32).reshape(slots, rows_x).astype(BF)
+    x_out[...] += dot(returned, onehot_cols(sends, atoms), TN)
+
+    for copy in halo_copies + chan_copies + near_copies + back_copies:
+        copy.wait_send()
+    for k in range(groups):
+        q = lax.rem(group + k, groups)
+
+        @pl.when(q != line)
+        def drain():
+            far_copy(k, q).wait_send()
+
+
+def call(kernel, outs, scratch=(), flops=10**8, collective=None):
+    if collective is None:
+        params = pltpu.CompilerParams(vmem_limit_bytes=VMEM_LIMIT)
+    else:
+        params = pltpu.CompilerParams(
+            vmem_limit_bytes=VMEM_LIMIT, collective_id=collective, has_side_effects=True
+        )
     return pl.pallas_call(
         kernel,
         out_shape=outs,
         scratch_shapes=list(scratch),
-        compiler_params=pltpu.CompilerParams(vmem_limit_bytes=VMEM_LIMIT),
+        compiler_params=params,
         cost_estimate=pl.CostEstimate(
             flops=flops, bytes_accessed=8 * 10**6, transcendentals=0
         ),
@@ -270,42 +601,112 @@
     slots = parts * halo
     rows = 49 * width
     share = channels // parts
-    exact = share % 16 != 0
+    fast = parts == 2 * groups and share % 16 == 0 and width == 2 * share
     sds = jax.ShapeDtypeStruct
 
     node = node_x.reshape(rows, atoms)
     cot = cotangent.reshape(rows, atoms)
+    factor = 1.0 / math.sqrt(edges * parts)
+    src = source.reshape(1, edges)
+    tgt = target.reshape(1, edges)
+    pad = lambda n: -(-n // LANES) * LANES
+    lz, l1, l2 = pad(7 * width), pad(12 * width), pad(10 * width)
+
+    if fast:
+        height = (7 * lz + 6 * l1 + 5 * l2) // LANES * share
+        vmem = pltpu.VMEM
+        dma = pltpu.SemaphoreType.DMA
+        grad_x, dz, d1, d2 = call(
+            functools.partial(whole_kernel, factor),
+            (
+                sds((rows, atoms), F32),
+                sds((7, 7, share, width), F32),
+                sds((2, 6, 6, share, width), F32),
+                sds((2, 5, 5, share, width), F32),
+            ),
+            (
+                vmem((parts, halo, rows), BF),
+                vmem((parts, halo, rows), BF),
+                vmem((groups, atoms, rows), BF),
+                vmem((235, edges), F32),
+                vmem((rows, edges), F32),
+                vmem((1, edges), F32),
+                vmem((7 * channels, edges), BF),
+                vmem((6 * channels, 2 * edges), BF),
+                vmem((5 * channels, 2 * edges), BF),
+                vmem((7 * width, edges), BF),
+                vmem((6 * width, 2 * edges), BF),
+                vmem((5 * width, 2 * edges), BF),
+                vmem((lz, edges), BF),
+                vmem((l1, 2 * edges), BF),
+                vmem((l2, 2 * edges), BF),
+                vmem((7 * width, 7 * channels), BF),
+                vmem((12 * width, 6 * channels), BF),
+                vmem((10 * width, 5 * channels), BF),
+                vmem((29 * width, edges), F32),
+                vmem((rows, edges), BF),
+                vmem((parts, halo, rows), BF),
+                vmem((parts, halo, rows), BF),
+                vmem((groups, 2, height, LANES), BF),
+                vmem((groups, height, LANES), BF),
+                vmem((groups, height, LANES), BF),
+                vmem((groups - 1, height, LANES), BF),
+                vmem((height, LANES), F32),
+                dma((parts,)),
+                dma((parts,)),
+                dma((groups,)),
+                dma((groups,)),
+                dma((groups,)),
+                dma((groups,)),
+                dma((groups,)),
+                dma((groups - 1,)),
+                dma((parts,)),
+                dma((parts,)),
+            ),
+            flops=10**10,
+            collective=0,
+        )(
+            send_index[0],
+            node,
+            cot,
+            rotation,
+            envelope.reshape(1, edges),
+            src,
+            tgt,
+            edge_count.reshape(1, 1),
+            halo_count.reshape(1, parts),
+            weight_zero.transpose(0, 2, 1, 3),
+            weight_one.transpose(0, 1, 3, 2, 4),
+            weight_two.transpose(0, 1, 3, 2, 4),
+        )
+        return (
+            grad_x.reshape(49, width, atoms),
+            dz.transpose(0, 3, 1, 2),
+            d1.transpose(0, 1, 4, 2, 3),
+            d2.transpose(0, 1, 4, 2, 3),
+        )
+
     sends = send_index.reshape(slots, 1)
     send_rows, cot_rows = call(
         prep_kernel, (sds((slots, rows), BF), sds((atoms, rows), BF))
     )(sends, node, cot)
     recv = lax.all_to_all(send_rows, "atoms", split_axis=0, concat_axis=0, tiled=True)
     cots = lax.all_gather(cot_rows, "chan", axis=0, tiled=False)
-
     valid = (
         jnp.arange(halo, dtype=jnp.int32)[None, :] < halo_count[:, 0][:, None]
     ).astype(F32).reshape(slots, 1)
-    src = source.reshape(1, edges)
-    tgt = target.reshape(1, edges)
-
     g_shapes = (
         sds((7 * channels, edges), BF),
         sds((6 * channels, 2 * edges), BF),
         sds((5 * channels, 2 * edges), BF),
     )
-    pad = lambda n: -(-n // LANES) * LANES
-    lz, l1, l2 = pad(7 * width), pad(12 * width), pad(10 * width)
-    height = (7 * lz + 6 * l1 + 5 * l2) // LANES * share
-    if exact:
-        d_shapes = (
-            sds((7 * channels, lz), F32),
-            sds((6 * channels, l1), F32),
-            sds((5 * channels, l2), F32),
-        )
-    else:
-        d_shapes = (sds((parts, height, LANES), BF),)
+    d_shapes = (
+        sds((7 * channels, lz), F32),
+        sds((6 * channels, l1), F32),
+        sds((5 * channels, l2), F32),
+    )
     made = call(
-        functools.partial(frame_kernel, exact),
+        frame_kernel,
         g_shapes + d_shapes,
         (
             pltpu.VMEM((235, edges), F32),
@@ -328,11 +729,6 @@
         valid,
     )
     gz, g1, g2 = made[:3]
-    factor = 1.0 / math.sqrt(edges * parts)
-
-    if not exact:
-        pieces = lax.all_to_all(made[3], "atoms", split_axis=0, concat_axis=0, tiled=True)
-
     own, halo_rows = call(
         back_kernel,
         (sds((rows, atoms), F32), sds((slots, rows), BF)),
@@ -355,28 +751,12 @@
     back = lax.all_to_all(halo_rows, "atoms", split_axis=0, concat_axis=0, tiled=True)
     grad_x = call(join_kernel, sds((rows, atoms), F32))(own, back, sends)
 
-    if exact:
-        dz = made[3][:, : 7 * width].reshape(7, channels, 7, width)
-        d1 = made[4].reshape(6, channels, 2, 6, width)
-        d2 = made[5][:, : 10 * width].reshape(5, channels, 2, 5, width)
-        dz = lax.psum_scatter(dz, "atoms", scatter_dimension=1, tiled=True)
-        d1 = lax.psum_scatter(d1, "atoms", scatter_dimension=1, tiled=True)
-        d2 = lax.psum_scatter(d2, "atoms", scatter_dimension=1, tiled=True)
-    else:
-        total = jnp.sum(pieces.astype(F32), axis=0)
-
-        def take(start, count_l, lanes):
-            tiles = lanes // LANES
-            size = count_l * share
-            got = [total[start + t * size : start + (t + 1) * size] for t in range(tiles)]
-            return jnp.concatenate(got, axis=1), start + tiles * size
-
-        dz, start = take(0, 7, lz)
-        d1, start = take(start, 6, l1)
-        d2, start = take(start, 5, l2)
-        dz = dz[:, : 7 * width].reshape(7, share, 7, width)
-        d1 = d1[:, : 12 * width].reshape(6, share, 2, 6, width)
-        d2 = d2[:, : 10 * width].reshape(5, share, 2, 5, width)
+    dz = made[3][:, : 7 * width].reshape(7, channels, 7, width)
+    d1 = made[4].reshape(6, channels, 2, 6, width)
+    d2 = made[5][:, : 10 * width].reshape(5, channels, 2, 5, width)
+    dz = lax.psum_scatter(dz, "atoms", scatter_dimension=1, tiled=True)
+    d1 = lax.psum_scatter(d1, "atoms", scatter_dimension=1, tiled=True)
+    d2 = lax.psum_scatter(d2, "atoms", scatter_dimension=1, tiled=True)
     return (
         grad_x.reshape(49, width, atoms),
         dz.transpose(2, 3, 0, 1) * factor,

time: 108 us -> 56 us (0.52)
  the two profiles are of different devices: /device:TPU:0 before, /device:TPU:2 now
where the time goes in v3:
time: 56 us; the launch traced here: 55.7 us
  Pallas kernels  49.1 us (88%)
  local copies, waits for them, and re-layouts  5.31 us (9%)
  between operations  1.3 us (2%)
    pallas_call x1, Pallas kernels, on_device(): call(functools.partial(whole_kernel, factor), (sds((rows, atoms), F32), s...  49.1 us
    unnamed x10, local copies, waits for them, and re-layouts  5.31 us

profile of v3, /device:TPU:2, one launch (start us, length us, event | category | flops | bytes accessed | tf_op | source)
XLA Modules:
  0.0 55.7 jit_solution(16723077585572840476)
XLA Ops:
  1.3 49.1 %shard_map.147 = (f32[1568,64]{1,0:T(8,128)}, f32[7,7,16,32]{3,2,1,0:T(8,128)}, f32[2,6,6,16,32]{4,3,2,1,0:T(8,128)}, f32[2,5,5,16,32]{4,3,2,1,0:T(8,128)}) custom-call(s32[8,8]{1,0:T(8,128)} %bitcast.25, bf16[1568,64]{1,0:T(8,128)(2,1)} %bitcast.22, bf16[1568,64]{1,0:T(8,128)(2,1)} %bitcast.23, bf16[235,512]{1,0:T(8,128)(2,1)} %rotation.1, ...), custom_call_target="tpu_custom_call" | custom-call | flops 10000000000 | bytes 8000000 | tf_op jit(solution)/shard_map/pallas_call | solution.py:619
  50.4 0.0 copy-start.2
  50.4 2.1 %copy.21 = f32[49,32,64]{2,1,0:T(8,128)} copy(f32[49,32,64]{2,1,0:T(8,128)} %bitcast.16) | data formatting | bytes 802816
  52.5 0.0 copy-done.2
  52.5 0.0 copy-start
  52.5 0.7 %copy.22 = f32[7,32,7,16]{1,3,2,0:T(8,128)} copy(f32[7,32,7,16]{1,3,2,0:T(8,128)S(1)} %bitcast.19) | data formatting | bytes 200704
  53.3 0.5 copy-done
  53.7 0.0 copy-start.1
  53.7 0.8 %copy.23 = f32[2,6,32,6,16]{2,4,3,1,0:T(8,128)} copy(f32[2,6,32,6,16]{2,4,3,1,0:T(8,128)S(1)} %bitcast.17) | data formatting | bytes 294912
  54.5 0.4 copy-done.1
  54.9 0.8 %copy.24 = f32[2,5,32,5,16]{2,4,3,1,0:T(8,128)} copy(f32[2,5,32,5,16]{2,4,3,1,0:T(8,128)S(1)} %bitcast.18) | data formatting | bytes 204800
Async XLA Ops:
  50.4 2.1 %copy-start.2 = (f32[7,7,16,32]{3,2,1,0:T(8,128)S(1)}, f32[7,7,16,32]{3,2,1,0:T(8,128)}, u32[]{:S(2)}) copy-start(f32[7,7,16,32]{3,2,1,0:T(8,128)} %get-tuple-element.9) | copy-start | bytes 301060
  52.5 1.2 %copy-start = (f32[2,6,6,16,32]{4,3,2,1,0:T(8,128)S(1)}, f32[2,6,6,16,32]{4,3,2,1,0:T(8,128)}, u32[]{:S(2)}) copy-start(f32[2,6,6,16,32]{4,3,2,1,0:T(8,128)} %get-tuple-element.10) | copy-start | bytes 442372
  53.7 1.2 %copy-start.1 = (f32[2,5,5,16,32]{4,3,2,1,0:T(8,128)S(1)}, f32[2,5,5,16,32]{4,3,2,1,0:T(8,128)}, u32[]{:S(2)}) copy-start(f32[2,5,5,16,32]{4,3,2,1,0:T(8,128)} %get-tuple-element.11) | copy-start | bytes 307204

commit v4 on v3

--- a/solution.py
+++ b/solution.py
@@ -247,9 +247,7 @@
     w1_in,
     w2_in,
     x_out,
-    dz_out,
-    d1_out,
-    d2_out,
+    total,
     mine,
     land,
     cots,
@@ -276,7 +274,6 @@
     near,
     passing,
     far,
-    total,
     halo_sent,
     halo_got,
     chan_sent,
@@ -499,13 +496,14 @@
         fb[pl.ds(start, rows), :] = real[:, :edges] + imag[:, edges:]
         fb[pl.ds(start + rows, rows), :] = real[:, edges:] - imag[:, :edges]
         start += 2 * rows
-    pass_on(groups - 1)
 
     def one_back(block, carry):
         rotate_out(rot, fb, block, width, y)
         return carry
 
-    lax.fori_loop(0, blocks, one_back, 0)
+    lax.fori_loop(0, blocks // 2, one_back, 0)
+    pass_on(groups - 1)
+    lax.fori_loop(blocks // 2, blocks, one_back, 0)
     terms = dot(remote, y[...], NT).astype(BF)
     for p in range(parts):
         back_mine[p] = terms[p * halo : (p + 1) * halo, :]
@@ -531,9 +529,30 @@
         ).wait_recv()
         value = value + far[j].astype(F32)
     total[...] = value * factor
+
+    for copy in back_copies:
+        copy.wait_recv()
+    returned = back_land[...].astype(F32).reshape(slots, rows_x).astype(BF)
+    x_out[...] += dot(returned, onehot_cols(sends, atoms), TN)
+
+    for copy in halo_copies + chan_copies + near_copies + back_copies:
+        copy.wait_send()
+    for k in range(groups):
+        q = lax.rem(group + k, groups)
+
+        @pl.when(q != line)
+        def drain():
+            far_copy(k, q).wait_send()
+
+
+def write_kernel(x, total, x_out, dz_out, d1_out, d2_out):
+    x_out[...] = x[...]
     base = 0
-    for c, (count_l, h, out) in enumerate(((7, hz, dz_out), (6, h1, d1_out), (5, h2, d2_out))):
-        for i in range(count_l if c == 0 else 2 * count_l):
+    for c, out in enumerate((dz_out, d1_out, d2_out)):
+        share, width = out.shape[-2:]
+        count_l = 7 - c
+        high = count_l if c == 0 else 2 * count_l
+        for i in range(high):
             tile, lane = divmod(i * width, LANES)
             for j in range(count_l):
                 row = base + (tile * count_l + j) * share
@@ -542,21 +561,7 @@
                     out[i, j] = cut
                 else:
                     out[i // count_l, i % count_l, j] = cut
-        base += h.shape[0] // LANES * count_l * share
-
-    for copy in back_copies:
-        copy.wait_recv()
-    returned = back_land[...].astype(F32).reshape(slots, rows_x).astype(BF)
-    x_out[...] += dot(returned, onehot_cols(sends, atoms), TN)
-
-    for copy in halo_copies + chan_copies + near_copies + back_copies:
-        copy.wait_send()
-    for k in range(groups):
-        q = lax.rem(group + k, groups)
-
-        @pl.when(q != line)
-        def drain():
-            far_copy(k, q).wait_send()
+        base += -(-high * width // LANES) * count_l * share
 
 
 def call(kernel, outs, scratch=(), flops=10**8, collective=None):
@@ -616,14 +621,9 @@
         height = (7 * lz + 6 * l1 + 5 * l2) // LANES * share
         vmem = pltpu.VMEM
         dma = pltpu.SemaphoreType.DMA
-        grad_x, dz, d1, d2 = call(
+        grad_x, summed = call(
             functools.partial(whole_kernel, factor),
-            (
-                sds((rows, atoms), F32),
-                sds((7, 7, share, width), F32),
-                sds((2, 6, 6, share, width), F32),
-                sds((2, 5, 5, share, width), F32),
-            ),
+            (sds((rows, atoms), F32), sds((height, LANES), F32)),
             (
                 vmem((parts, halo, rows), BF),
                 vmem((parts, halo, rows), BF),
@@ -651,7 +651,6 @@
                 vmem((groups, height, LANES), BF),
                 vmem((groups, height, LANES), BF),
                 vmem((groups - 1, height, LANES), BF),
-                vmem((height, LANES), F32),
                 dma((parts,)),
                 dma((parts,)),
                 dma((groups,)),
@@ -679,6 +678,15 @@
             weight_one.transpose(0, 1, 3, 2, 4),
             weight_two.transpose(0, 1, 3, 2, 4),
         )
+        grad_x, dz, d1, d2 = call(
+            write_kernel,
+            (
+                sds((rows, atoms), F32),
+                sds((7, 7, share, width), F32),
+                sds((2, 6, 6, share, width), F32),
+                sds((2, 5, 5, share, width), F32),
+            ),
+        )(grad_x, summed)
         return (
             grad_x.reshape(49, width, atoms),
             dz.transpose(0, 3, 1, 2),

time: 56 us -> 53 us (0.946)
  local copies, waits for them, and re-layouts: 5.31 us -> 0 us
  Pallas kernels: 49.1 us -> 51.5 us
    unnamed x10 -> x0, local copies, waits for them, and re-layouts: 5.31 us -> none
    pallas_call x0 -> x1, Pallas kernels: none -> 2.83 us  [on_device(): call(write_kernel, (sds((rows, atoms), F32), sds((7, 7, share, width), F3...]
where the time goes in v4:
time: 53 us; the launch traced here: 52.8 us
  Pallas kernels  51.5 us (97%)
  between operations  1.29 us (2%)
    pallas_call x1, Pallas kernels, on_device(): call(functools.partial(whole_kernel, factor), (sds((rows, atoms), F32), s...  48.7 us
    pallas_call x1, Pallas kernels, on_device(): call(write_kernel, (sds((rows, atoms), F32), sds((7, 7, share, width), F3...  2.83 us

profile of v4, /device:TPU:2, one launch (start us, length us, event | category | flops | bytes accessed | tf_op | source)
XLA Modules:
  0.0 52.8 jit_solution(576043641446160930)
XLA Ops:
  1.3 48.7 %shard_map.147 = (f32[1568,64]{1,0:T(8,128)}, f32[752,128]{1,0:T(8,128)}) custom-call(s32[8,8]{1,0:T(8,128)} %bitcast.25, bf16[1568,64]{1,0:T(8,128)(2,1)} %bitcast.21, bf16[1568,64]{1,0:T(8,128)(2,1)} %bitcast.22, bf16[235,512]{1,0:T(8,128)(2,1)} %rotation.1, f32[1,512]{1,0:T(1,128)} %bitcast.26, s32[1,512]{1,0:T(1,128)} %bitcast.27, s32[1,512]{1,0:T(1,128)} %bitcast.28, ...), custom_call_target="tpu_custom_call" | custom-call | flops 10000000000 | bytes 8000000 | tf_op jit(solution)/shard_map/pallas_call | solution.py:624
  50.0 2.8 %shard_map.148 = (f32[1568,64]{1,0:T(8,128)}, f32[7,7,16,32]{3,2,1,0:T(8,128)}, f32[2,6,6,16,32]{4,3,2,1,0:T(8,128)}, f32[2,5,5,16,32]{4,3,2,1,0:T(8,128)}) custom-call(f32[1568,64]{1,0:T(8,128)} %get-tuple-element.10.x, f32[752,128]{1,0:T(8,128)} %get-tuple-element.11.total), custom_call_target="tpu_custom_call" | custom-call | flops 100000000 | bytes 8000000 | tf_op jit(solution)/shard_map/pallas_call | solution.py:681
